TPU v7x, 128 devices: a whole 4x4x4 slice. The times are simulated.
128 devices in a mesh: dom: 16 (over y, z), sub: 8 (over x, core).
Axes of the slice: x: 4, y: 4, z: 4, core: 2. Of those that a mesh axis runs over, the one named last changes fastest.
Arguments:
- charges: bfloat16 [65536, 1152], P(('dom', 'sub')), may hold values from -6 to 6
- frac_coords: float32 [3, 65536], P(None, ('dom', 'sub')), may hold values from 0 to 1
- atom_counts: int32 [128], replicated, may hold values from 0 to 512, as said below
- miller: int32 [3, 4096], replicated, may hold values from -10 to 10, as said below
- box: float32 [3], replicated, may hold values from 200 to 400
- cotangent: float32 [128], replicated, may hold values from 0.25 to 4
Outputs:
- grad_charges: float32 [65536, 1152], P(('dom', 'sub'))
- grad_coords: float32 [3, 65536], P(None, ('dom', 'sub'))
Inputs may be any that keep to these rules, and one draw needn't show every extreme that they name: `atom_counts`: the counts sum to 32768; some sub-domain holds exactly 512 atoms and some none. `miller`: the k-vectors are distinct and the third index of every k-vector is 1 or more, so no k-vector is zero.
All inputs are finite; a program needn't handle non-finite values.
Results may differ from a plain program's by a relative error of at most 0.005.
Values may be sent and summed in bfloat16 or wider, within the bound.
No kernel may reach another device: no remote copies, remote signals or barrier semaphores. Data moves between devices by JAX's collectives and lax.ppermute only.
A program may use at most 64 MiB of HBM per device.

v0:
```python
import math

import jax
import jax.numpy as jnp
from jax import lax
from jax.sharding import PartitionSpec as P

RECV = 256


TWO_PI = 2.0 * math.pi
ROOT_THREE = math.sqrt(3.0)


def split_up(x, dim, devices):
    before, after = (x.shape[:dim], x.shape[dim + 1 :])
    return jnp.moveaxis(x.reshape(*before, devices, -1, *after), dim, 0)


def summed_on_arrival(x, axis, dim):
    devices = lax.axis_size(axis)
    blocks = lax.all_to_all(split_up(x, dim, devices), axis, 0, 0, tiled=True)
    return jnp.sum(blocks, axis=0)


def joined_along(blocks, dim):
    blocks = jnp.moveaxis(blocks, 0, dim)
    lengths = blocks.shape
    return blocks.reshape(*lengths[:dim], lengths[dim] * lengths[dim + 1], *lengths[dim + 2 :])


def from_everyone(x, axis):
    devices = lax.axis_size(axis)
    return lax.all_to_all(jnp.broadcast_to(x[None], (devices, *x.shape)), axis, 0, 0, tiled=True)


def collect(x, axis, dim):
    return joined_along(from_everyone(x, axis), dim)


def sent_together(arrays, axis, split_dim, concat_dim, along):
    both = jnp.concatenate(arrays, axis=along)
    whole, at, finished = (
        lax.all_to_all(both, axis, split_axis=split_dim, concat_axis=concat_dim, tiled=True),
        0,
        [],
    )
    for a in arrays:
        finished.append(lax.slice_in_dim(whole, at, at + a.shape[along], axis=along))
        at += a.shape[along]
    return tuple(finished)


def unit_tables(miller, box):
    k_vectors = TWO_PI * miller.astype(jnp.float32) / box[:, None]
    k_square = jnp.sum(k_vectors * k_vectors, axis=0)
    inverse = 1.0 / jnp.sqrt(k_square)
    unit_x = k_vectors[0] * inverse
    unit_y = k_vectors[1] * inverse
    unit_z = k_vectors[2] * inverse
    zero_row = jnp.zeros_like(unit_x)
    ones_row = jnp.ones_like(unit_x)
    even_table = jnp.stack(
        [
            ones_row,
            zero_row,
            zero_row,
            zero_row,
            -ROOT_THREE * unit_x * unit_y,
            -ROOT_THREE * unit_y * unit_z,
            -ROOT_THREE * unit_z * unit_x,
            -0.5 * ROOT_THREE * (unit_x * unit_x - unit_y * unit_y),
            -0.5 * (3.0 * unit_z * unit_z - 1.0),
        ],
        axis=0,
    )
    odd_table = jnp.stack(
        [zero_row, unit_x, unit_y, unit_z, zero_row, zero_row, zero_row, zero_row, zero_row], axis=0
    )
    k_filter = jnp.exp(-0.5 * k_square) / k_square
    return (even_table, odd_table, k_filter)


def split_coords(fraction):
    coarse = fraction.astype(jnp.bfloat16)
    coarse_back = lax.optimization_barrier(coarse).astype(jnp.float32)
    fine_part = (fraction - coarse_back).astype(jnp.bfloat16)
    return jnp.concatenate([coarse, fine_part], axis=0).T


def phase_tiles(coords, k_nums):
    fraction = coords[:, 0:3].astype(jnp.float32) + coords[:, 3:6].astype(jnp.float32)
    numbers = k_nums.astype(jnp.float32)
    angle = TWO_PI * (
        fraction[:, 0:1] * numbers[0][None, :]
        + fraction[:, 1:2] * numbers[1][None, :]
        + fraction[:, 2:3] * numbers[2][None, :]
    )
    return (jnp.cos(angle).astype(jnp.bfloat16), jnp.sin(angle).astype(jnp.bfloat16))


def k_blocks(miller, even_table, odd_table):
    k_count = miller.shape[1]
    k_block = min(k_count, 256)
    block_count = k_count // k_block
    return (
        miller.reshape(3, block_count, k_block).transpose(1, 0, 2),
        even_table.reshape(9, block_count, k_block).transpose(1, 0, 2),
        odd_table.reshape(9, block_count, k_block).transpose(1, 0, 2),
    )


def structure_partial(charges, coords, miller, even_table, odd_table):
    row_width = charges.shape[1]
    channels = row_width // 9
    k_count = miller.shape[1]
    k_block = min(k_count, 256)
    highest = lax.Precision.HIGHEST

    def structure_one_block(inputs):
        k_nums, k_even, k_odd = inputs
        cosine, sine = phase_tiles(coords, k_nums)
        cos_q = jnp.dot(cosine.T, charges, preferred_element_type=jnp.float32).reshape(
            k_block, 9, channels
        )
        sin_q = jnp.dot(sine.T, charges, preferred_element_type=jnp.float32).reshape(
            k_block, 9, channels
        )
        real_part = jnp.einsum("mk,kmc->kc", k_even, cos_q, precision=highest) - jnp.einsum(
            "mk,kmc->kc", k_odd, sin_q, precision=highest
        )
        imag_part = jnp.einsum("mk,kmc->kc", k_even, sin_q, precision=highest) + jnp.einsum(
            "mk,kmc->kc", k_odd, cos_q, precision=highest
        )
        return jnp.stack([real_part, imag_part], axis=1)

    blocks = lax.map(structure_one_block, k_blocks(miller, even_table, odd_table))
    return blocks.reshape(k_count, 2, channels)


def scaled_factors(summed, k_filter, cotangent, atom_total, filter_norm):
    weight = k_filter / (filter_norm * jnp.sqrt(atom_total))
    return (summed * weight[:, None, None] * cotangent[None, None, :]).astype(jnp.bfloat16)


def gradient_rows(charges, coords, miller, even_table, odd_table, factor):
    row_count, row_width = charges.shape
    channels = row_width // 9
    k_count = miller.shape[1]
    k_block = min(k_count, 256)
    block_count = k_count // k_block
    highest = lax.Precision.HIGHEST
    nums_b, even_b, odd_b = k_blocks(miller, even_table, odd_table)
    factor_b = factor.reshape(block_count, k_block, 2, channels)

    def gradient_one_block(running, inputs):
        grad_q, grad_f = running
        k_nums, k_even, k_odd, k_factor = inputs
        cosine, sine = phase_tiles(coords, k_nums)
        real_wide = k_factor[:, 0, :].astype(jnp.float32)[:, None, :]
        imag_wide = k_factor[:, 1, :].astype(jnp.float32)[:, None, :]
        even_t = k_even.T[:, :, None]
        odd_t = k_odd.T[:, :, None]
        cos_coef = (
            (even_t * real_wide + odd_t * imag_wide)
            .astype(jnp.bfloat16)
            .reshape(k_block, row_width)
        )
        sin_coef = (
            (even_t * imag_wide - odd_t * real_wide)
            .astype(jnp.bfloat16)
            .reshape(k_block, row_width)
        )
        grad_q = (
            grad_q
            + jnp.dot(cosine, cos_coef, preferred_element_type=jnp.float32)
            + jnp.dot(sine, sin_coef, preferred_element_type=jnp.float32)
        )
        with_sin = jnp.dot(charges, sin_coef.T, preferred_element_type=jnp.float32)
        with_cos = jnp.dot(charges, cos_coef.T, preferred_element_type=jnp.float32)
        turning = cosine.astype(jnp.float32) * with_sin - sine.astype(jnp.float32) * with_cos
        grad_f = grad_f + TWO_PI * jnp.dot(turning, k_nums.astype(jnp.float32).T, precision=highest)
        return ((grad_q, grad_f), None)

    start = (jnp.zeros((row_count, row_width), jnp.float32), jnp.zeros((row_count, 3), jnp.float32))
    (grad_q, grad_f), ignored = lax.scan(
        gradient_one_block, start, (nums_b, even_b, odd_b, factor_b)
    )
    return (grad_q, grad_f)


def local(charges, frac_coords, atom_counts, miller, box, cotangent):
    dom_count = lax.axis_size("dom")
    sub_count = lax.axis_size("sub")
    devices = dom_count * sub_count
    my_index = lax.axis_index(("dom", "sub"))
    cap_rows, row_width = charges.shape
    channels = row_width // 9
    k_count = miller.shape[1]
    coords = split_coords(frac_coords)
    even_table, odd_table, k_filter = unit_tables(miller, box)
    filter_norm = jnp.sqrt(jnp.sum(k_filter * k_filter))
    atom_total = jnp.sum(atom_counts).astype(jnp.float32)
    starts = jnp.cumsum(atom_counts) - atom_counts
    my_count = atom_counts[my_index]
    my_start = starts[my_index]
    row_index = jnp.arange(cap_rows, dtype=jnp.int32)
    is_live = row_index < my_count
    per_peer = cap_rows // devices
    slot_index = jnp.arange(per_peer, dtype=jnp.int32)[None, :]
    peer_index = jnp.arange(devices, dtype=jnp.int32)[:, None]
    local_row = (peer_index - my_start) % devices + slot_index * devices
    sent_live = (local_row < my_count).reshape(-1)
    pick_rows = jnp.where(sent_live, local_row.reshape(-1), 0)
    send_q = jnp.where(sent_live[:, None], charges[pick_rows], jnp.zeros((), jnp.bfloat16))
    send_c = jnp.where(sent_live[:, None], coords[pick_rows], jnp.zeros((), jnp.bfloat16))
    arrived_q, arrived_c = (
        lax.all_to_all(send_q, ("dom", "sub"), split_axis=0, concat_axis=0, tiled=True),
        lax.all_to_all(send_c, ("dom", "sub"), split_axis=0, concat_axis=0, tiled=True),
    )
    source_row = (my_index - starts[:, None]) % devices + slot_index * devices
    came_live = (source_row < atom_counts[:, None]).reshape(-1)
    slot_rank = jnp.cumsum(came_live.astype(jnp.int32)) - 1
    target = jnp.where(came_live, slot_rank, RECV)
    picked = (
        jnp.zeros((RECV,), jnp.int32)
        .at[target]
        .set(jnp.arange(cap_rows, dtype=jnp.int32), mode="drop")
    )
    work_q = arrived_q[picked]
    work_c = arrived_c[picked]
    summed_part = structure_partial(work_q, work_c, miller, even_table, odd_table)
    channel_part = lax.psum_scatter(summed_part, "sub", scatter_dimension=2, tiled=True)
    owned = summed_on_arrival(channel_part, "dom", 0)
    k_share = k_count // dom_count
    c_share = channels // sub_count
    share_filter = lax.dynamic_slice_in_dim(k_filter, lax.axis_index("dom") * k_share, k_share)
    share_cotangent = lax.dynamic_slice_in_dim(cotangent, lax.axis_index("sub") * c_share, c_share)
    owned_factor = scaled_factors(owned, share_filter, share_cotangent, atom_total, filter_norm)
    k_factor = collect(owned_factor, "dom", 0)
    factor = lax.all_gather(k_factor, "sub", axis=2, tiled=True)
    grad_q, grad_f = gradient_rows(work_q, work_c, miller, even_table, odd_table, factor)
    back_q = jnp.zeros((cap_rows, row_width), jnp.float32).at[picked].set(grad_q)
    back_f = jnp.zeros((cap_rows, 3), jnp.float32).at[picked].set(grad_f)
    returned_q, returned_f = sent_together((back_q, back_f), ("dom", "sub"), 0, 0, 1)
    home_row = (my_start + row_index) % devices * per_peer + row_index // devices
    grad_q = returned_q[home_row]
    grad_f = returned_f[home_row]
    out_q = jnp.where(is_live[:, None], grad_q, 0.0)
    out_f = jnp.where(is_live[:, None], grad_f, 0.0)
    return (out_q, out_f.T)


def solution(mesh):
    in_specs = (P(("dom", "sub"), None), P(None, ("dom", "sub")), P(), P(), P(), P())
    out_specs = (P(("dom", "sub"), None), P(None, ("dom", "sub")))
    return jax.shard_map(local, mesh=mesh, in_specs=in_specs, out_specs=out_specs, check_vma=False)
```

profile of v0, /device:TPU:1, one launch (start us, length us, event | category | flops | bytes accessed | tf_op | source)
XLA Modules:
  0.0 531.5 jit_solution(16808649420633809437)
XLA Ops:
  12.3 1.9 broadcast_compare_fusion
  18.6 11.9 %all-to-all-start = ((bf16[128,4,6]{2,1,0:T(4,128)(2,1)}), bf16[128,4,6]{2,1,0:T(4,128)(2,1)}, u32[]{:S(2)}, u32[]{:S(2)}) async-start(bf16[128,4,6]{2,1,0:T(4,128)(2,1)} %broadcast_select_fusion.2), calls=%async_computation | async-start | bytes 262144 | tf_op jit(solution)/shard_map/all_to_all | solution.py:219
  31.9 2.1 gather_fusion.2
  34.4 1.6 broadcast_select_fusion.1
  38.2 2.4 scatter_custom_fusion
  41.0 10.2 %all-to-all-start.1 = ((bf16[128,4,1152]{2,1,0:T(4,128)(2,1)}), bf16[128,4,1152]{2,1,0:T(4,128)(2,1)}, u32[]{:S(2)}, u32[]{:S(2)}) async-start(bf16[128,4,1152]{2,1,0:T(4,128)(2,1)} %broadcast_select_fusion.1), calls=%async_computation.1 | async-start | bytes 2359296 | tf_op jit(solution)/shard_map/all_to_all | solution.py:218
  51.8 1.6 gather_fusion.1
  53.5 18.0 %all-to-all-done.1 = bf16[128,4,1152]{2,1,0:T(4,128)(2,1)} async-done(((bf16[128,4,1152]{2,1,0:T(4,128)(2,1)}), bf16[128,4,1152]{2,1,0:T(4,128)(2,1)}, u32[]{:S(2)}, u32[]{:S(2)}) %all-to-all-start.1) | async-done | bytes 1179680 | tf_op jit(solution)/shard_map/all_to_all | solution.py:218
  71.6 2.4 all_to_all.29
  75.2 82.9 %while.23 = (s32[]{:T(128)}, f32[16,256,2,128]{3,2,1,0:T(2,128)}, f32[16,9,256]{2,1,0:T(8,128)S(1)}, bf16[256,6]{0,1:T(8,128)(2,1)S(1)}, s32[16,3,256]{2,1,0:T(4...) while((s32[]{:T(128)}, f32[16,256,2,128]{3,2,1,0:T(2,128)}, ...), condition=%wide.region_6.7_spmd, body=%wide.region_5.6_spmd.sunk | while | flops 305269760 | bytes 8874589 | solution.py:137
  107.0 1.3 fusion.81
  127.7 1.3 fusion.81
  132.9 1.3 fusion.81
  143.3 1.3 fusion.81
  158.1 8.7 %copy.109 = f32[4096,2,128]{0,1,2:T(2,128)} copy(f32[4096,2,128]{2,1,0:T(2,128)} %bitcast.190) | data formatting | bytes 8388608 | tf_op jit(solution)/shard_map/reshape | solution.py:138
  168.7 64.9 %all-reduce.3.cloned.1.call-done = f32[4096,2,128]{0,1,2:T(2,128)} async-done(((f32[4096,2,128]{0,1,2:T(2,128)}), f32[4096,2,128]{0,1,2:T(2,128)}) %all-reduce.3.cloned.1.call-update) | async-done | bytes 4194320
  236.3 6.7 %all-to-all-start.2 = ((f32[16,256,2,16]{1,3,2,0:T(8,128)}), f32[16,256,2,16]{1,3,2,0:T(8,128)S(1)}, u32[]{:S(2)}, u32[]{:S(2)}) async-start(f32[16,256,2,16]{1,3,2,0:T(8,128)} %copy.73), calls=%async_computation.2 | async-start | bytes 1048576 | tf_op jit(solution)/shard_map/all_to_all | solution.py:22
  244.5 7.7 %all-to-all-done.2 = f32[16,256,2,16]{1,3,2,0:T(8,128)S(1)} async-done(((f32[16,256,2,16]{1,3,2,0:T(8,128)}), f32[16,256,2,16]{1,3,2,0:T(8,128)S(1)}, u32[]{:S(2)}, u32[]{:S(2)}) %all-to-all-start.2) | async-done | bytes 524320 | tf_op jit(solution)/shard_map/all_to_all | solution.py:22
  252.3 10.4 %all_to_all.40 = bf16[16,256,2,16]{1,3,2,0:T(8,128)(2,1)S(1)} all-to-all(bf16[16,256,2,16]{1,3,2,0:T(8,128)(2,1)S(1)} %broadcast_in_dim.109), channel_id=1, replica_groups=mesh['dom'=16,'sub'=8] {'dom'}, dimensions={0} | all-to-all | bytes 524288 | tf_op jit(solution)/shard_map/all_to_all | solution.py:34
  263.6 27.9 %all-gather.2.cloned.1.call-done = bf16[4096,2,128]{0,1,2:T(2,128)(2,1)} async-done(((bf16[4096,2,16]{0,1,2:T(2,128)(2,1)}), bf16[4096,2,128]{0,1,2:T(2,128)(2,1)}) %all-gather.2.cloned.1.call-update) | async-done | bytes 2097168 | tf_op jit(solution)/shard_map/all_gather | solution.py:241
  291.5 6.2 %copy.78 = bf16[4096,2,128]{2,0,1:T(8,128)(2,1)} copy(bf16[4096,2,128]{0,1,2:T(2,128)(2,1)} %all-gather.2.cloned.1.call-done) | data formatting | bytes 4194304 | tf_op jit(solution)/shard_map/all_gather | solution.py:241
  297.6 155.8 %while.24 = (s32[]{:T(128)}, f32[256,1152]{1,0:T(8,128)}, f32[256,3]{0,1:T(4,128)S(1)}, bf16[256,6]{0,1:T(8,128)(2,1)S(1)}, s32[16,3,256]{2,1,0:T(4,128)}, /*ind...) while((s32[]{:T(128)}, f32[256,1152]{1,0:T(8,128)}, ...), condition=%wide.region_12.13_spmd.clone, body=%wide.region_11.12_spmd.clone.sunk | while | flops 611816704 | bytes 11779204 | solution.py:186
  301.1 2.4 convolution_add_fusion.5
  308.3 2.6 convolution_add_fusion.4
  310.9 2.4 convolution_add_fusion.5
  318.1 2.6 convolution_add_fusion.4
  320.7 2.4 convolution_add_fusion.5
  327.9 2.6 convolution_add_fusion.4
  330.5 2.4 convolution_add_fusion.5
  337.8 2.6 convolution_add_fusion.4
  340.4 2.4 convolution_add_fusion.5
  347.6 2.6 convolution_add_fusion.4
  350.2 2.4 convolution_add_fusion.5
  357.4 2.6 convolution_add_fusion.4
  360.0 2.4 convolution_add_fusion.5
  367.2 2.6 convolution_add_fusion.4
  369.8 2.4 convolution_add_fusion.5
  377.0 2.6 convolution_add_fusion.4
  379.6 2.4 convolution_add_fusion.5
  386.9 2.6 convolution_add_fusion.4
  389.5 2.4 convolution_add_fusion.5
  396.7 2.6 convolution_add_fusion.4
  399.3 2.4 convolution_add_fusion.5
  406.5 2.6 convolution_add_fusion.4
  409.1 2.4 convolution_add_fusion.5
  416.3 2.6 convolution_add_fusion.4
  418.9 2.4 convolution_add_fusion.5
  426.1 2.6 convolution_add_fusion.4
  428.7 2.4 convolution_add_fusion.5
  435.9 2.6 convolution_add_fusion.4
  438.6 2.4 convolution_add_fusion.5
  445.8 2.6 convolution_add_fusion.4
  448.4 2.4 convolution_add_fusion.5
  453.4 2.7 scatter_custom_fusion.1
  457.0 2.2 scatter_custom_fusion.2
  459.2 2.7 pad_maximum_fusion
  461.8 3.9 all_to_all.32
  465.7 8.7 %all-to-all-start.4 = ((f32[128,4,1155]{2,1,0:T(4,128)}), f32[128,4,1155]{2,1,0:T(4,128)}, u32[]{:S(2)}, u32[]{:S(2)}) async-start(f32[128,4,1155]{2,1,0:T(4,128)} %all_to_all.32), calls=%async_computation.4 | async-start | bytes 5242880 | tf_op jit(solution)/shard_map/all_to_all | solution.py:44
  475.7 34.5 %all-to-all-done.4 = f32[128,4,1155]{2,1,0:T(4,128)} async-done(((f32[128,4,1155]{2,1,0:T(4,128)}), f32[128,4,1155]{2,1,0:T(4,128)}, u32[]{:S(2)}, u32[]{:S(2)}) %all-to-all-start.4) | async-done | bytes 2365472 | tf_op jit(solution)/shard_map/all_to_all | solution.py:44
  510.2 4.0 all_to_all.34
  514.2 1.7 copy-done.1
  516.6 2.9 gather_fusion.4
  519.5 2.7 gather_fusion.5
  522.2 1.6 broadcast_select_fusion
  (534 shorter events, 177.7 us)
Async XLA Ops:
  7.2 24.8 %copy-start = (bf16[512,1152]{1,0:T(8,128)(2,1)S(1)}, bf16[512,1152]{1,0:T(8,128)(2,1)}, u32[]{:S(2)}) copy-start(bf16[512,1152]{1,0:T(8,128)(2,1)} %param.10) | copy-start | bytes 3538948
  7.2 8.4 %copy-start.9 = (s32[4]{0:T(128)}, s32[4]{0:T(128)S(1)}, u32[]{:S(2)}) copy-start(s32[4]{0:T(128)S(1)} %iota_multiply_fusion) | copy-start | bytes 52
  7.2 24.0 %copy-start.6 = (s32[128]{0:T(128)S(1)}, s32[128]{0:T(128)}, u32[]{:S(2)}) copy-start(s32[128]{0:T(128)} %param.12) | copy-start | bytes 1540
  18.6 22.4 %all-to-all-start = ((bf16[128,4,6]{2,1,0:T(4,128)(2,1)}), bf16[128,4,6]{2,1,0:T(4,128)(2,1)}, u32[]{:S(2)}, u32[]{:S(2)}) async-start(bf16[128,4,6]{2,1,0:T(4,128)(2,1)} %broadcast_select_fusion.2), calls=%async_computation | async-start | bytes 262144 | tf_op jit(solution)/shard_map/all_to_all | solution.py:219
  34.4 1.7 copy-start.5
  34.4 1.8 copy-start.8
  34.4 2.0 copy-start.10
  34.4 2.1 copy-start.7
  34.4 2.9 copy-start.4
  34.4 2.9 copy-start.11
  41.0 30.5 %all-to-all-start.1 = ((bf16[128,4,1152]{2,1,0:T(4,128)(2,1)}), bf16[128,4,1152]{2,1,0:T(4,128)(2,1)}, u32[]{:S(2)}, u32[]{:S(2)}) async-start(bf16[128,4,1152]{2,1,0:T(4,128)(2,1)} %broadcast_select_fusion.1), calls=%async_computation.1 | async-start | bytes 2359296 | tf_op jit(solution)/shard_map/all_to_all | solution.py:218
  51.2 182.4 %all-reduce.3.cloned.1.call-start = ((), (), s32[]{:S(2)}) async-start(), calls=%async_computation.6 | async-start | bytes 8388608
  166.8 0.7 copy-start.13
  235.1 9.2 %copy-start.12 = (f32[128]{0:T(128)S(1)}, f32[128]{0:T(128)}, u32[]{:S(2)}) copy-start(f32[128]{0:T(128)} %param.15) | copy-start | bytes 1540
  236.3 15.9 %all-to-all-start.2 = ((f32[16,256,2,16]{1,3,2,0:T(8,128)}), f32[16,256,2,16]{1,3,2,0:T(8,128)S(1)}, u32[]{:S(2)}, u32[]{:S(2)}) async-start(f32[16,256,2,16]{1,3,2,0:T(8,128)} %copy.73), calls=%async_computation.2 | async-start | bytes 1048576 | tf_op jit(solution)/shard_map/all_to_all | solution.py:22
  243.0 48.5 %all-gather.2.cloned.1.call-start = ((), (), s32[]{:S(2)}) async-start(), calls=%async_computation.5 | async-start | bytes 2359296 | tf_op jit(solution)/shard_map/all_gather | solution.py:241
  465.7 44.4 %all-to-all-start.4 = ((f32[128,4,1155]{2,1,0:T(4,128)}), f32[128,4,1155]{2,1,0:T(4,128)}, u32[]{:S(2)}, u32[]{:S(2)}) async-start(f32[128,4,1155]{2,1,0:T(4,128)} %all_to_all.32), calls=%async_computation.4 | async-start | bytes 5242880 | tf_op jit(solution)/shard_map/all_to_all | solution.py:44
  514.2 1.7 copy-start.1
  514.2 2.5 slice-start
  519.5 2.7 copy-start.2
  522.2 1.6 copy-start.3
Sparse Core Ops, SparseCore 0:
  166.9 66.6 all-reduce.2
  263.7 27.7 all-gather.1
where the time goes:
time: 535 us; the launch traced here: 532 us
  matrix products  164 us (31%)
  waiting for transfers between devices  153 us (29%)
  local copies, waits for them, and re-layouts  82.6 us (15%)
  other arithmetic  64.9 us (12%)
  starting transfers between devices  37.8 us (7%)
  between operations  16.5 us (3%)
  blocking collectives  10.4 us (2%)
    unnamed x3, waiting for transfers between devices  65 us
    dot_general x16, matrix products, gradient_one_block(): jnp.dot(cosine, cos_coef, preferred_element_type=jnp.float32)  40.4 us
    dot_general x16, matrix products, gradient_one_block(): jnp.dot(sine, sin_coef, preferred_element_type=jnp.float32)  38 us
    all_to_all x1, waiting for transfers between devices, sent_together(): lax.all_to_all(both, axis, split_axis=split_dim, concat_axis=concat_dim,...  34.5 us
    all_gather x1, waiting for transfers between devices, local(): factor = lax.all_gather(k_factor, 'sub', axis=2, tiled=True)  27.9 us
    convert_element_type x32, other arithmetic, phase_tiles(): numbers = k_nums.astype(jnp.float32)  22.1 us
    dot_general x16, matrix products, structure_one_block(): jnp.dot(sine.T, charges, preferred_element_type=jnp.float32)  21.5 us
    dot_general x16, matrix products, structure_one_block(): jnp.dot(cosine.T, charges, preferred_element_type=jnp.float32)  21.4 us
  transfers between devices with their start and end apart: 6, of which 5 were waited for; matrix products, arithmetic and copies ran while one was open for 3% of the time, Pallas kernels for 0%

commit v1 on v0

v1 whole, which is shorter than its diff:
```python
import functools
import math

import jax
import jax.numpy as jnp
from jax import lax
from jax.experimental import pallas as pl
from jax.experimental.pallas import tpu as pltpu
from jax.sharding import PartitionSpec as P

TWO_PI = 2.0 * math.pi
ROOT_THREE = math.sqrt(3.0)
MULT = 9
EVEN = (0, 4, 5, 6, 7, 8)
ODD = (1, 2, 3)

SIN_TERMS = (
    4.442883014678955,
    -7.308241367340088,
    3.6062889099121094,
    -0.8457635641098022,
    0.10920575261116028,
)
COS_TERMS = (
    1.4142135381698608,
    -6.978850841522217,
    5.7394609451293945,
    -1.8835630416870117,
    0.31069818139076233,
)


def series(terms, x):
    total = terms[-1]
    for term in terms[-2::-1]:
        total = total * x + term
    return total


def turned(columns, rows):
    turns = columns[0] * rows[0] + columns[1] * rows[1] + columns[2] * rows[2]
    rest = turns - jnp.round(turns)
    square = rest * rest
    half_sin = rest * series(SIN_TERMS, square)
    half_cos = series(COS_TERMS, square)
    cosine = 1.0 - half_sin * half_sin
    sine = half_sin * half_cos
    return cosine.astype(jnp.bfloat16), sine.astype(jnp.bfloat16)


def squared_k(numbers, box_ref):
    parts = [TWO_PI * numbers[x] / box_ref[x] for x in range(3)]
    return parts, parts[0] * parts[0] + parts[1] * parts[1] + parts[2] * parts[2]


def harmonic_rows(numbers, box_ref):
    parts, k_square = squared_k(numbers, box_ref)
    inverse = 1.0 / jnp.sqrt(k_square)
    ux, uy, uz = (part * inverse for part in parts)
    rows = {
        0: None,
        1: ux,
        2: uy,
        3: uz,
        4: -ROOT_THREE * ux * uy,
        5: -ROOT_THREE * uy * uz,
        6: -ROOT_THREE * uz * ux,
        7: -0.5 * ROOT_THREE * (ux * ux - uy * uy),
        8: -0.5 * (3.0 * uz * uz - 1.0),
    }
    return rows, k_square


def times(row, x):
    return x if row is None else row * x


def number_rows(miller_ref, start, width):
    return [
        miller_ref[x : x + 1, pl.ds(start, width)].astype(jnp.float32) for x in range(3)
    ]


def structure_kernel(
    k_block,
    box_ref,
    charges_ref,
    frac_ref,
    counts_ref,
    miller_ref,
    cotangent_ref,
    part_ref,
    phases_ref,
    charges_t,
    columns,
    gain,
    cos_sums,
    sin_sums,
):
    step = pl.program_id(0)
    rows, width = charges_ref.shape
    channels = width // MULT
    k_count = miller_ref.shape[1]
    subs = part_ref.shape[0]
    me = lax.axis_index("dom") * lax.axis_size("sub") + lax.axis_index("sub")

    @pl.when(step == 0)
    def _():
        counts = counts_ref[...]
        lane = lax.broadcasted_iota(jnp.int32, counts.shape, 1)
        mine = jnp.sum(jnp.where(lane == me, counts, 0), axis=1, keepdims=True)
        total = jnp.sum(counts, axis=1, keepdims=True).astype(jnp.float32)
        live = lax.broadcasted_iota(jnp.int32, (rows, 1), 0) < mine
        charges = jnp.where(live, charges_ref[...].astype(jnp.float32), 0.0)
        charges_t[...] = charges.T.astype(jnp.bfloat16)
        coords = frac_ref[...]
        coarse = coords.astype(jnp.bfloat16).astype(jnp.float32)
        fine = (coords - coarse).astype(jnp.bfloat16).astype(jnp.float32)
        position = coarse + fine
        padded = jnp.concatenate([position, jnp.zeros((5, rows), jnp.float32)], axis=0)
        columns[...] = padded.T
        all_numbers = number_rows(miller_ref, 0, k_count)
        _, all_square = squared_k(all_numbers, box_ref)
        all_filter = jnp.exp(-0.5 * all_square) / all_square
        norm = jnp.sqrt(jnp.sum(all_filter * all_filter, axis=1, keepdims=True))
        cotangent = jnp.broadcast_to(cotangent_ref[...], (8, channels)).T[:, 0:1]
        gain[...] = cotangent / (norm * jnp.sqrt(total))

    start = pl.multiple_of(step * k_block, k_block)
    numbers = number_rows(miller_ref, start, k_block)
    table, k_square = harmonic_rows(numbers, box_ref)
    k_filter = jnp.exp(-0.5 * k_square) / k_square
    position = [columns[:, x : x + 1] for x in range(3)]
    cosine, sine = turned(position, numbers)
    phases_ref[0, 0] = cosine
    phases_ref[0, 1] = sine
    cos_sums[...] = jnp.dot(charges_t[...], cosine, preferred_element_type=jnp.float32)
    sin_sums[...] = jnp.dot(charges_t[...], sine, preferred_element_type=jnp.float32)
    share = channels // subs
    for s in range(subs):
        real_part = imag_part = None
        for m in range(MULT):
            at = pl.ds(m * channels + s * share, share)
            with_cos = times(table[m], cos_sums[at, :])
            with_sin = times(table[m], sin_sums[at, :])
            if m in ODD:
                with_cos, with_sin = -with_sin, with_cos
            real_part = with_cos if real_part is None else real_part + with_cos
            imag_part = with_sin if imag_part is None else imag_part + with_sin
        scale = gain[s * share : (s + 1) * share, :] * k_filter
        part_ref[s, 0, 0] = (real_part * scale).astype(jnp.bfloat16)
        part_ref[s, 0, 1] = (imag_part * scale).astype(jnp.bfloat16)


def gradient_kernel(
    k_block,
    box_ref,
    charges_ref,
    counts_ref,
    miller_ref,
    factor_ref,
    phases_ref,
    grad_q_ref,
    grad_f_ref,
    cos_coef,
    sin_coef,
    turned_by,
):
    step = pl.program_id(0)
    rows, width = charges_ref.shape
    channels = width // MULT
    subs = factor_ref.shape[0]
    me = lax.axis_index("dom") * lax.axis_size("sub") + lax.axis_index("sub")

    @pl.when(step == 0)
    def _():
        grad_q_ref[...] = jnp.zeros_like(grad_q_ref)
        turned_by[...] = jnp.zeros_like(turned_by)

    start = pl.multiple_of(step * k_block, k_block)
    numbers = number_rows(miller_ref, start, k_block)
    table, _ = harmonic_rows(numbers, box_ref)
    share = channels // subs
    for s in range(subs):
        real = factor_ref[s, 0, 0].astype(jnp.float32)
        imag = factor_ref[s, 0, 1].astype(jnp.float32)
        for m in range(MULT):
            at = pl.ds(m * channels + s * share, share)
            first, second = (imag, -real) if m in ODD else (real, imag)
            cos_coef[at, :] = times(table[m], first).astype(jnp.bfloat16)
            sin_coef[at, :] = times(table[m], second).astype(jnp.bfloat16)
    charges = charges_ref[...]
    with_sin = jnp.dot(charges, sin_coef[...], preferred_element_type=jnp.float32)
    with_cos = jnp.dot(charges, cos_coef[...], preferred_element_type=jnp.float32)
    cosine = phases_ref[0, 0]
    sine = phases_ref[0, 1]
    turning = cosine.astype(jnp.float32) * with_sin - sine.astype(jnp.float32) * with_cos
    for x in range(3):
        moved = turning * numbers[x]
        folded = moved[:, 0:128]
        for at in range(128, k_block, 128):
            folded = folded + moved[:, at : at + 128]
        turned_by[x] += folded
    contract = (((1,), (1,)), ((), ()))
    grad_q_ref[...] += lax.dot_general(
        cosine, cos_coef[...], contract, preferred_element_type=jnp.float32
    ) + lax.dot_general(sine, sin_coef[...], contract, preferred_element_type=jnp.float32)

    @pl.when(step == pl.num_programs(0) - 1)
    def _():
        counts = counts_ref[...]
        lane = lax.broadcasted_iota(jnp.int32, counts.shape, 1)
        mine = jnp.sum(jnp.where(lane == me, counts, 0), axis=1, keepdims=True)
        live = lax.broadcasted_iota(jnp.int32, (rows, 1), 0) < mine
        grad_q_ref[...] = jnp.where(live, grad_q_ref[...], 0.0)
        live_lane = lax.broadcasted_iota(jnp.int32, (1, rows), 1) < mine
        for x in range(3):
            moved = TWO_PI * jnp.sum(turned_by[x].T, axis=0, keepdims=True)
            grad_f_ref[x : x + 1, :] = jnp.where(live_lane, moved, 0.0)


def whole(shape):
    return pl.BlockSpec(shape, lambda j: (0,) * len(shape))


SMEM = pl.BlockSpec(memory_space=pltpu.SMEM)


def local(charges, frac_coords, atom_counts, miller, box, cotangent):
    doms = lax.axis_size("dom")
    subs = lax.axis_size("sub")
    rows, width = charges.shape
    channels = width // MULT
    k_count = miller.shape[1]
    k_block = k_count // doms
    share = channels // subs
    counts = atom_counts[None, :]
    part, phases = pl.pallas_call(
        functools.partial(structure_kernel, k_block),
        grid=(doms,),
        in_specs=[
            SMEM,
            whole((rows, width)),
            whole((3, rows)),
            whole((1, doms * subs)),
            whole((3, k_count)),
            whole((1, channels)),
        ],
        out_specs=[
            pl.BlockSpec((subs, 1, 2, share, k_block), lambda j: (0, j, 0, 0, 0)),
            pl.BlockSpec((1, 2, rows, k_block), lambda j: (j, 0, 0, 0)),
        ],
        out_shape=[
            jax.ShapeDtypeStruct((subs, doms, 2, share, k_block), jnp.bfloat16),
            jax.ShapeDtypeStruct((doms, 2, rows, k_block), jnp.bfloat16),
        ],
        scratch_shapes=[
            pltpu.VMEM((width, rows), jnp.bfloat16),
            pltpu.VMEM((rows, 8), jnp.float32),
            pltpu.VMEM((channels, 1), jnp.float32),
            pltpu.VMEM((width, k_block), jnp.float32),
            pltpu.VMEM((width, k_block), jnp.float32),
        ],
        name="structure",
    )(box, charges, frac_coords, counts, miller, cotangent[None, :])
    arrived = lax.all_to_all(part, "sub", 0, 0, tiled=True)
    over_sub = jnp.sum(arrived.astype(jnp.float32), axis=0).astype(jnp.bfloat16)
    arrived = lax.all_to_all(over_sub, "dom", 0, 0, tiled=True)
    factor = jnp.sum(arrived.astype(jnp.float32), axis=0).astype(jnp.bfloat16)
    factor = lax.all_gather(factor, "dom", axis=0, tiled=False)
    factor = lax.all_gather(factor, "sub", axis=0, tiled=False)
    grad_q, grad_f = pl.pallas_call(
        functools.partial(gradient_kernel, k_block),
        grid=(doms,),
        in_specs=[
            SMEM,
            whole((rows, width)),
            whole((1, doms * subs)),
            whole((3, k_count)),
            pl.BlockSpec((subs, 1, 2, share, k_block), lambda j: (0, j, 0, 0, 0)),
            pl.BlockSpec((1, 2, rows, k_block), lambda j: (j, 0, 0, 0)),
        ],
        out_specs=[whole((rows, width)), whole((3, rows))],
        out_shape=[
            jax.ShapeDtypeStruct((rows, width), jnp.float32),
            jax.ShapeDtypeStruct((3, rows), jnp.float32),
        ],
        scratch_shapes=[
            pltpu.VMEM((width, k_block), jnp.bfloat16),
            pltpu.VMEM((width, k_block), jnp.bfloat16),
            pltpu.VMEM((3, rows, 128), jnp.float32),
        ],
        name="gradient",
    )(box, charges, counts, miller, factor, phases)
    return grad_q, grad_f


def solution(mesh):
    in_specs = (P(("dom", "sub"), None), P(None, ("dom", "sub")), P(), P(), P(), P())
    out_specs = (P(("dom", "sub"), None), P(None, ("dom", "sub")))
    return jax.shard_map(local, mesh=mesh, in_specs=in_specs, out_specs=out_specs, check_vma=False)
```

time: 535 us -> 162 us (0.30)
  matrix products: 164 us -> 0 us
  waiting for transfers between devices: 153 us -> 29.4 us
  local copies, waits for them, and re-layouts: 82.6 us -> 0 us
  other arithmetic: 64.9 us -> 0.41 us
  blocking collectives: 10.4 us -> 65.7 us
  Pallas kernels: 0 us -> 51.8 us
  starting transfers between devices: 37.8 us -> 0.04 us
    dot_general x112 -> x0, matrix products: 164 us -> none  [the longest x16 40.4 us: gradient_one_block(): jnp.dot(cosine, cos_coef, preferred_element_type=jnp.float32)]
    unnamed x3 -> x1, waiting for transfers between devices: 65 us -> 0.02 us
    all_to_all x4 -> x0, waiting for transfers between devices: 60.2 us -> none  [the longest x1 34.5 us: sent_together(): lax.all_to_all(both, axis, split_axis=split_dim, concat_axis=concat_dim,...]
    pallas_call x0 -> x2, Pallas kernels: none -> 51.8 us  [the longest x1 30.2 us: local(): pl.pallas_call(functools.partial(gradient_kernel, k_block), grid=(doms,),...]
    all_to_all x4 -> x0, starting transfers between devices: 37.5 us -> none  [the longest x1 11.9 us: local(): lax.all_to_all(send_c, ('dom', 'sub'), split_axis=0, concat_axis=0, tiled...]
    all_to_all x1 -> x2, blocking collectives: 10.4 us -> 47 us  [the longest x1 32 us: local(): arrived = lax.all_to_all(part, 'sub', 0, 0, tiled=True)]
    convert_element_type x52 -> x0, other arithmetic: 28.7 us -> none  [the longest x32 22.1 us: phase_tiles(): numbers = k_nums.astype(jnp.float32)]
    all_gather x0 -> x1, blocking collectives: none -> 18.7 us  [local(): factor = lax.all_gather(factor, 'dom', axis=0, tiled=False)]
  transfers between devices with their start and end apart: 6 -> 1, of which waited for: 5 -> 1; matrix products, arithmetic and copies ran while one was open for 3% -> 0% of each run, Pallas kernels for 0% -> 0%
where the time goes in v1:
time: 162 us; the launch traced here: 161 us
  blocking collectives  65.7 us (41%)
  Pallas kernels  51.8 us (32%)
  waiting for transfers between devices  29.4 us (18%)
  between operations  14 us (9%)
    all_to_all x1, blocking collectives, local(): arrived = lax.all_to_all(part, 'sub', 0, 0, tiled=True)  32 us
    pallas_call x1, Pallas kernels, local(): pl.pallas_call(functools.partial(gradient_kernel, k_block), grid=(doms,),...  30.2 us
    all_gather x1, waiting for transfers between devices, local(): factor = lax.all_gather(factor, 'sub', axis=0, tiled=False)  29.4 us
    pallas_call x1, Pallas kernels, local(): pl.pallas_call(functools.partial(structure_kernel, k_block), grid=(doms,)...  21.6 us
    all_gather x1, blocking collectives, local(): factor = lax.all_gather(factor, 'dom', axis=0, tiled=False)  18.7 us
    all_to_all x1, blocking collectives, local(): arrived = lax.all_to_all(over_sub, 'dom', 0, 0, tiled=True)  15 us
  transfers between devices with their start and end apart: 1, of which 1 were waited for; matrix products, arithmetic and copies ran while one was open for 0% of the time, Pallas kernels for 0%

profile of v1, /device:TPU:1, one launch (start us, length us, event | category | flops | bytes accessed | tf_op | source)
XLA Modules:
  0.0 161.4 jit_solution(18352105357642613087)
XLA Ops:
  7.2 0.0 all-gather.4.cloned.1.call-start
  7.2 21.6 %structure.1 = (bf16[8,16,2,16,256]{4,3,2,1,0:T(8,128)(2,1)}, bf16[16,2,512,256]{3,2,1,0:T(8,128)(2,1)}) custom-call(f32[3]{0:T(128)} %box_ref.3, bf16[512,1152]{1,0:T(8,128)(2,1)} %charges_ref.3, f32[3,512]{1,0:T(4,128)} %frac_ref.1, s32[1,128]{1,0:T(1,128)} %bitcast.6, s32[3,4096]{1,0:T(4,128)} %miller_ref.3, f32[1,128]{1,0:T(1,128)} %bitcast.8), custom_call_target="tpu_custom_call" | custom-call | tf_op jit(solution)/shard_map/structure/pallas_call | solution.py:238
  28.8 32.0 %all_to_all.10 = bf16[8,16,2,16,256]{4,3,2,1,0:T(8,128)(2,1)S(1)} all-to-all(bf16[8,16,2,16,256]{4,3,2,1,0:T(8,128)(2,1)} %get-tuple-element.4), channel_id=1, replica_groups=mesh['dom'=16,'sub'=8] {'sub'}, dimensions={0} | all-to-all | bytes 4194304 | tf_op jit(solution)/shard_map/all_to_all | solution.py:266
  60.8 0.4 reduce_sum.24
  61.2 15.0 %all_to_all.11 = bf16[16,2,16,256]{3,2,1,0:T(8,128)(2,1)S(1)} all-to-all(bf16[16,2,16,256]{3,2,1,0:T(8,128)(2,1)S(1)} %reduce_sum.24), channel_id=1, replica_groups=mesh['dom'=16,'sub'=8] {'dom'}, dimensions={0} | all-to-all | bytes 524288 | tf_op jit(solution)/shard_map/all_to_all | solution.py:268
  76.2 18.7 %all-gather = bf16[32,16,256]{2,1,0:T(8,128)(2,1)} all-gather(bf16[2,16,256]{2,1,0:T(8,128)(2,1)S(1)} %reduce_sum.25), channel_id=2, replica_groups=mesh['dom'=16,'sub'=8] {'dom'}, dimensions={0}, use_global_device_ids=true | all-gather | bytes 278528 | tf_op jit(solution)/shard_map/all_gather | solution.py:270
  94.9 0.0 all-gather.4.cloned.1.call-update
  94.9 29.4 %all-gather.4.cloned.1.call-done = bf16[128,2,16,256]{3,2,1,0:T(8,128)(2,1)} async-done(((bf16[16,2,16,256]{3,2,1,0:T(8,128)(2,1)}), bf16[128,2,16,256]{3,2,1,0:T(8,128)(2,1)}) %all-gather.4.cloned.1.call-update) | async-done | bytes 2097168 | tf_op jit(solution)/shard_map/all_gather | solution.py:271
  124.3 30.2 %gradient.1 = (f32[512,1152]{1,0:T(8,128)}, f32[3,512]{1,0:T(4,128)}) custom-call(f32[3]{0:T(128)} %box_ref.3, bf16[512,1152]{1,0:T(8,128)(2,1)} %charges_ref.3, s32[1,128]{1,0:T(1,128)} %bitcast.7, s32[3,4096]{1,0:T(4,128)} %miller_ref.3, bf16[8,16,2,16,256]{4,3,2,1,0:T(8,128)(2,1)} %bitcast.4, bf16[16,2,512,256]{3,2,1,0:T(8,128)(2,1)} %get-tuple-element.5.phases_ref), custom_call_target="tpu_custom_call" | custom-call | tf_op jit(solution)/shard_map/gradient/pallas_call | solution.py:272
  (1 shorter events, 0.0 us)
Async XLA Ops:
  7.2 117.2 %all-gather.4.cloned.1.call-start = ((), (), s32[]{:S(2)}) async-start(), calls=%async_computation.2 | async-start | bytes 2359296 | tf_op jit(solution)/shard_map/all_gather | solution.py:271
Sparse Core Ops, SparseCore 0:
  95.1 29.2 all-gather.3

commit v2 on v1

v2 whole, which is shorter than its diff:
```python
import functools
import math

import jax
import jax.numpy as jnp
from jax import lax
from jax.experimental import pallas as pl
from jax.experimental.pallas import tpu as pltpu
from jax.sharding import PartitionSpec as P

TWO_PI = 2.0 * math.pi
ROOT_THREE = math.sqrt(3.0)
MULT = 9
EVEN = (0, 4, 5, 6, 7, 8)
ODD = (1, 2, 3)

SIN_TERMS = (
    4.442883014678955,
    -7.308241367340088,
    3.6062889099121094,
    -0.8457635641098022,
    0.10920575261116028,
)
COS_TERMS = (
    1.4142135381698608,
    -6.978850841522217,
    5.7394609451293945,
    -1.8835630416870117,
    0.31069818139076233,
)


def series(terms, x):
    total = terms[-1]
    for term in terms[-2::-1]:
        total = total * x + term
    return total


def turned(columns, rows):
    turns = columns[0] * rows[0] + columns[1] * rows[1] + columns[2] * rows[2]
    rest = turns - jnp.round(turns)
    square = rest * rest
    half_sin = rest * series(SIN_TERMS, square)
    half_cos = series(COS_TERMS, square)
    cosine = 1.0 - half_sin * half_sin
    sine = half_sin * half_cos
    return cosine.astype(jnp.bfloat16), sine.astype(jnp.bfloat16)


def squared_k(numbers, box_ref):
    parts = [TWO_PI * numbers[x] / box_ref[x] for x in range(3)]
    return parts, parts[0] * parts[0] + parts[1] * parts[1] + parts[2] * parts[2]


def harmonic_rows(numbers, box_ref):
    parts, k_square = squared_k(numbers, box_ref)
    inverse = 1.0 / jnp.sqrt(k_square)
    ux, uy, uz = (part * inverse for part in parts)
    rows = {
        0: None,
        1: ux,
        2: uy,
        3: uz,
        4: -ROOT_THREE * ux * uy,
        5: -ROOT_THREE * uy * uz,
        6: -ROOT_THREE * uz * ux,
        7: -0.5 * ROOT_THREE * (ux * ux - uy * uy),
        8: -0.5 * (3.0 * uz * uz - 1.0),
    }
    return rows, k_square


def times(row, x):
    return x if row is None else row * x


def number_rows(miller_ref, start, width):
    return [
        miller_ref[x : x + 1, pl.ds(start, width)].astype(jnp.float32) for x in range(3)
    ]


def live_rows(counts, me, shape, dim):
    lane = lax.broadcasted_iota(jnp.int32, counts.shape, 1)
    mine = jnp.sum(jnp.where(lane == me, counts, 0), axis=1, keepdims=True)
    return lax.broadcasted_iota(jnp.int32, shape, dim) < mine


def my_device():
    return lax.axis_index("dom") * lax.axis_size("sub") + lax.axis_index("sub")


def my_core():
    return lax.rem(lax.axis_index("sub"), 2)


def structure_kernel(
    k_block,
    box_ref,
    charges_ref,
    frac_ref,
    counts_ref,
    miller_ref,
    cotangent_ref,
    mine_ref,
    theirs_ref,
    phases_ref,
    charges_t,
    columns,
    gain,
    phases_0,
    phases_1,
    sums_0,
    sums_1,
):
    step = pl.program_id(0)
    rows, width = charges_ref.shape
    channels = width // MULT
    half = channels // 2
    k_count = miller_ref.shape[1]
    core = my_core()

    def block_numbers(block):
        start = pl.multiple_of(jnp.minimum(block * k_block, k_count - k_block), k_block)
        return number_rows(miller_ref, start, k_block)

    def write_phases(block, to):
        position = [columns[:, x : x + 1] for x in range(3)]
        cosine, sine = turned(position, block_numbers(block))
        to[0] = cosine
        to[1] = sine

    @pl.when(step == 0)
    def _():
        counts = counts_ref[...]
        total = jnp.sum(counts, axis=1, keepdims=True).astype(jnp.float32)
        live = live_rows(counts, my_device(), (rows, 1), 0)
        charges = jnp.where(live, charges_ref[...].astype(jnp.float32), 0.0)
        charges_t[...] = charges.T.astype(jnp.bfloat16)
        coords = frac_ref[...]
        coarse = coords.astype(jnp.bfloat16).astype(jnp.float32)
        fine = (coords - coarse).astype(jnp.bfloat16).astype(jnp.float32)
        position = coarse + fine
        padded = jnp.concatenate([position, jnp.zeros((5, rows), jnp.float32)], axis=0)
        columns[...] = padded.T
        all_numbers = number_rows(miller_ref, 0, k_count)
        _, all_square = squared_k(all_numbers, box_ref)
        all_filter = jnp.exp(-0.5 * all_square) / all_square
        norm = jnp.sqrt(jnp.sum(all_filter * all_filter, axis=1, keepdims=True))
        cotangent = jnp.broadcast_to(cotangent_ref[...], (8, channels)).T[:, 0:1]
        gain[...] = cotangent / (norm * jnp.sqrt(total))
        write_phases(0, phases_0)

    def one_block(part, phases, sums, following, other):
        block = 2 * step + part
        table, k_square = harmonic_rows(block_numbers(block), box_ref)
        k_filter = jnp.exp(-0.5 * k_square) / k_square
        sums[0] = jnp.dot(charges_t[...], phases[0], preferred_element_type=jnp.float32)
        sums[1] = jnp.dot(charges_t[...], phases[1], preferred_element_type=jnp.float32)
        phases_ref[part, 0] = phases[0]
        phases_ref[part, 1] = phases[1]
        write_phases(following, other)
        for ref, owner in ((mine_ref, core), (theirs_ref, 1 - core)):
            for at in range(0, half, 16):
                real_part = imag_part = None
                for m in range(MULT):
                    start = pl.multiple_of(m * channels + owner * half + at, 16)
                    with_cos = times(table[m], sums[0, pl.ds(start, 16), :])
                    with_sin = times(table[m], sums[1, pl.ds(start, 16), :])
                    if m in ODD:
                        with_cos, with_sin = -with_sin, with_cos
                    real_part = with_cos if real_part is None else real_part + with_cos
                    imag_part = with_sin if imag_part is None else imag_part + with_sin
                scale = gain[pl.ds(pl.multiple_of(owner * half + at, 16), 16), :] * k_filter
                ref[part, 0, at : at + 16] = (real_part * scale).astype(ref.dtype)
                ref[part, 1, at : at + 16] = (imag_part * scale).astype(ref.dtype)

    one_block(0, phases_0, sums_0, 2 * step + 1, phases_1)
    one_block(1, phases_1, sums_1, 2 * step + 2, phases_0)


def gradient_kernel(
    k_block,
    box_ref,
    charges_ref,
    counts_ref,
    miller_ref,
    mine_ref,
    theirs_ref,
    phases_ref,
    grad_q_ref,
    grad_f_ref,
    cos_coef,
    sin_coef,
    turned_by,
):
    step = pl.program_id(0)
    rows, width = charges_ref.shape
    channels = width // MULT
    half = channels // 2
    core = my_core()

    @pl.when(step == 0)
    def _():
        grad_q_ref[...] = jnp.zeros_like(grad_q_ref)
        turned_by[...] = jnp.zeros_like(turned_by)

    start = pl.multiple_of(step * k_block, k_block)
    numbers = number_rows(miller_ref, start, k_block)
    table, _ = harmonic_rows(numbers, box_ref)
    for ref, owner in ((mine_ref, core), (theirs_ref, 1 - core)):
        for at in range(0, half, 16):
            real = ref[0, 0, at : at + 16].astype(jnp.float32)
            imag = ref[0, 1, at : at + 16].astype(jnp.float32)
            for m in range(MULT):
                start = pl.multiple_of(m * channels + owner * half + at, 16)
                first, second = (imag, -real) if m in ODD else (real, imag)
                cos_coef[pl.ds(start, 16), :] = times(table[m], first).astype(jnp.bfloat16)
                sin_coef[pl.ds(start, 16), :] = times(table[m], second).astype(jnp.bfloat16)
    charges = charges_ref[...]
    with_sin = jnp.dot(charges, sin_coef[...], preferred_element_type=jnp.float32)
    with_cos = jnp.dot(charges, cos_coef[...], preferred_element_type=jnp.float32)
    cosine = phases_ref[0, 0]
    sine = phases_ref[0, 1]
    turning = cosine.astype(jnp.float32) * with_sin - sine.astype(jnp.float32) * with_cos
    for x in range(3):
        moved = turning * numbers[x]
        folded = moved[:, 0:128]
        for at in range(128, k_block, 128):
            folded = folded + moved[:, at : at + 128]
        turned_by[x] += folded
    contract = (((1,), (1,)), ((), ()))
    grad_q_ref[...] += lax.dot_general(
        cosine, cos_coef[...], contract, preferred_element_type=jnp.float32
    ) + lax.dot_general(sine, sin_coef[...], contract, preferred_element_type=jnp.float32)

    @pl.when(step == pl.num_programs(0) - 1)
    def _():
        live = live_rows(counts_ref[...], my_device(), (rows, 1), 0)
        grad_q_ref[...] = jnp.where(live, grad_q_ref[...], 0.0)
        live_lane = live_rows(counts_ref[...], my_device(), (1, rows), 1)
        for x in range(3):
            moved = TWO_PI * jnp.sum(turned_by[x].T, axis=0, keepdims=True)
            grad_f_ref[x : x + 1, :] = jnp.where(live_lane, moved, 0.0)


def whole(shape):
    return pl.BlockSpec(shape, lambda j: (0,) * len(shape))


SMEM = pl.BlockSpec(memory_space=pltpu.SMEM)


def neighbours(doms, subs, moved):
    return [
        (dom * subs + sub, dom * subs + moved(sub)) for dom in range(doms) for sub in range(subs)
    ]


def local(charges, frac_coords, atom_counts, miller, box, cotangent):
    axes = ("dom", "sub")
    doms = lax.axis_size("dom")
    subs = lax.axis_size("sub")
    rows, width = charges.shape
    channels = width // MULT
    half = channels // 2
    k_count = miller.shape[1]
    k_block = k_count // doms
    counts = atom_counts[None, :]
    share = (doms, 2, half, k_block)
    share_pair = pl.BlockSpec((2, 2, half, k_block), lambda j: (j, 0, 0, 0))
    mine, theirs, phases = pl.pallas_call(
        functools.partial(structure_kernel, k_block),
        grid=(doms // 2,),
        in_specs=[
            SMEM,
            whole((rows, width)),
            whole((3, rows)),
            whole((1, doms * subs)),
            whole((3, k_count)),
            whole((1, channels)),
        ],
        out_specs=[
            share_pair,
            share_pair,
            pl.BlockSpec((2, 2, rows, k_block), lambda j: (j, 0, 0, 0)),
        ],
        out_shape=[
            jax.ShapeDtypeStruct(share, jnp.float32),
            jax.ShapeDtypeStruct(share, jnp.bfloat16),
            jax.ShapeDtypeStruct((doms, 2, rows, k_block), jnp.bfloat16),
        ],
        scratch_shapes=[
            pltpu.VMEM((width, rows), jnp.bfloat16),
            pltpu.VMEM((rows, 8), jnp.float32),
            pltpu.VMEM((channels, 1), jnp.float32),
            pltpu.VMEM((2, rows, k_block), jnp.bfloat16),
            pltpu.VMEM((2, rows, k_block), jnp.bfloat16),
            pltpu.VMEM((2, width, k_block), jnp.float32),
            pltpu.VMEM((2, width, k_block), jnp.float32),
        ],
        name="structure",
    )(box, charges, frac_coords, counts, miller, cotangent[None, :])
    other_core = neighbours(doms, subs, lambda sub: sub ^ 1)
    along_x = [
        neighbours(doms, subs, lambda sub, by=by: (sub + by) % subs) for by in range(2, subs, 2)
    ]
    arrived = lax.ppermute(theirs, axes, other_core)
    on_chip = (mine + arrived.astype(jnp.float32)).astype(jnp.bfloat16)
    arrived = lax.all_to_all(on_chip, "dom", 0, 0, tiled=True)
    summed = jnp.sum(arrived.astype(jnp.float32), axis=0)
    sent = summed.astype(jnp.bfloat16)
    for pairs in along_x:
        summed = summed + lax.ppermute(sent, axes, pairs).astype(jnp.float32)
    factor = summed.astype(jnp.bfloat16)
    mine = lax.all_to_all(jnp.broadcast_to(factor[None], share), "dom", 0, 0, tiled=True)
    theirs = lax.ppermute(mine, axes, other_core)
    share_one = pl.BlockSpec((1, 2, half, k_block), lambda j: (j, 0, 0, 0))
    grad_q, grad_f = pl.pallas_call(
        functools.partial(gradient_kernel, k_block),
        grid=(doms,),
        in_specs=[
            SMEM,
            whole((rows, width)),
            whole((1, doms * subs)),
            whole((3, k_count)),
            share_one,
            share_one,
            pl.BlockSpec((1, 2, rows, k_block), lambda j: (j, 0, 0, 0)),
        ],
        out_specs=[whole((rows, width)), whole((3, rows))],
        out_shape=[
            jax.ShapeDtypeStruct((rows, width), jnp.float32),
            jax.ShapeDtypeStruct((3, rows), jnp.float32),
        ],
        scratch_shapes=[
            pltpu.VMEM((width, k_block), jnp.bfloat16),
            pltpu.VMEM((width, k_block), jnp.bfloat16),
            pltpu.VMEM((3, rows, 128), jnp.float32),
        ],
        name="gradient",
    )(box, charges, counts, miller, mine, theirs, phases)
    return grad_q, grad_f


def solution(mesh):
    in_specs = (P(("dom", "sub"), None), P(None, ("dom", "sub")), P(), P(), P(), P())
    out_specs = (P(("dom", "sub"), None), P(None, ("dom", "sub")))
    return jax.shard_map(local, mesh=mesh, in_specs=in_specs, out_specs=out_specs, check_vma=False)
```

time: 162 us -> 117 us (0.72)
  blocking collectives: 65.7 us -> 40.5 us
  waiting for transfers between devices: 29.4 us -> 8.98 us
  between operations: 14 us -> 0.67 us
  starting transfers between devices: 0.04 us -> 9.83 us
  other arithmetic: 0.41 us -> 2.18 us
    all_gather x1 -> x0, waiting for transfers between devices: 29.4 us -> none  [local(): factor = lax.all_gather(factor, 'sub', axis=0, tiled=False)]
    all_gather x1 -> x0, blocking collectives: 18.7 us -> none  [local(): factor = lax.all_gather(factor, 'dom', axis=0, tiled=False)]
    ppermute x0 -> x5, starting transfers between devices: none -> 9.83 us  [the longest x1 4.78 us: local(): theirs = lax.ppermute(mine, axes, other_core)]
    ppermute x0 -> x5, waiting for transfers between devices: none -> 8.98 us  [the longest x3 4.2 us: local(): summed = summed + lax.ppermute(sent, axes, pairs).astype(jnp.float32)]
    all_to_all x2, blocking collectives: 47 us -> 40.5 us  [the longest x1 23.7 us: local(): arrived = lax.all_to_all(on_chip, 'dom', 0, 0, tiled=True)]
    convert_element_type x0 -> x3, other arithmetic: none -> 2.03 us  [the longest x1 1.98 us: local(): on_chip = (mine + arrived.astype(jnp.float32)).astype(jnp.bfloat16)]
    pallas_call x1, Pallas kernels: 30.2 us -> 31.9 us  [local(): pl.pallas_call(functools.partial(gradient_kernel, k_block), grid=(doms,),...]
  transfers between devices with their start and end apart: 1 -> 5, of which waited for: 1 -> 5; matrix products, arithmetic and copies ran while one was open for 0% -> 0% of each run, Pallas kernels for 0% -> 0%
where the time goes in v2:
time: 117 us; the launch traced here: 116 us
  Pallas kernels  53.1 us (45%)
  blocking collectives  40.5 us (35%)
  starting transfers between devices  9.83 us (8%)
  waiting for transfers between devices  8.98 us (8%)
  other arithmetic  2.18 us (2%)
    pallas_call x1, Pallas kernels, local(): pl.pallas_call(functools.partial(gradient_kernel, k_block), grid=(doms,),...  31.9 us
    all_to_all x1, blocking collectives, local(): arrived = lax.all_to_all(on_chip, 'dom', 0, 0, tiled=True)  23.7 us
    pallas_call x1, Pallas kernels, local(): pl.pallas_call(functools.partial(structure_kernel, k_block), grid=(doms /...  21.2 us
    all_to_all x1, blocking collectives, local(): lax.all_to_all(jnp.broadcast_to(factor[None], share), 'dom', 0, 0, tiled=...  16.8 us
    ppermute x1, starting transfers between devices, local(): theirs = lax.ppermute(mine, axes, other_core)  4.78 us
    ppermute x3, waiting for transfers between devices, local(): summed = summed + lax.ppermute(sent, axes, pairs).astype(jnp.float32)  4.2 us
    ppermute x3, starting transfers between devices, local(): summed = summed + lax.ppermute(sent, axes, pairs).astype(jnp.float32)  3.67 us
    ppermute x1, waiting for transfers between devices, local(): arrived = lax.ppermute(theirs, axes, other_core)  2.5 us
  transfers between devices with their start and end apart: 5, of which 5 were waited for; matrix products, arithmetic and copies ran while one was open for 0% of the time, Pallas kernels for 0%

profile of v2, /device:TPU:1, one launch (start us, length us, event | category | flops | bytes accessed | tf_op | source)
XLA Modules:
  0.0 116.3 jit_solution(17340250735881049234)
XLA Ops:
  0.6 21.2 %structure.1 = (f32[16,2,64,256]{3,2,1,0:T(8,128)}, bf16[16,2,64,256]{3,2,1,0:T(8,128)(2,1)}, bf16[16,2,512,256]{3,2,1,0:T(8,128)(2,1)}) custom-call(f32[3]{0:T(128)} %box_ref.3, bf16[512,1152]{1,0:T(8,128)(2,1)} %charges_ref.3, f32[3,512]{1,0:T(4,128)} %frac_ref.1, s32[1,128]{1,0:T(1,128)} %bitcast.2, s32[3,4096]{1,0:T(4,128)} %miller_ref.3, f32[1,128]{1,0:T(1,128)} %bitcast.4), custom_call_target="tpu_custom_call" | custom-call | tf_op jit(solution)/shard_map/structure/pallas_call | solution.py:273
  21.8 1.4 %collective-permute-start = (bf16[16,2,64,256]{3,2,1,0:T(8,128)(2,1)}, bf16[16,2,64,256]{3,2,1,0:T(8,128)(2,1)S(1)}, u32[]{:S(2)}, u32[]{:S(2)}) collective-permute-start(bf16[16,2,64,256]{3,2,1,0:T(8,128)(2,1)} %get-tuple-element.6), channel_id=1, source_target_pairs={{0,1},{1,0},{2,3},{3,2},{4,5},{5,4},{6,7},{7,6},{8,9},{9,8},{10,11... | collective-permute-start | bytes 3145736 | tf_op jit(solution)/shard_map/ppermute | solution.py:309
  23.2 2.5 %collective-permute-done = bf16[16,2,64,256]{3,2,1,0:T(8,128)(2,1)S(1)} collective-permute-done((bf16[16,2,64,256]{3,2,1,0:T(8,128)(2,1)}, bf16[16,2,64,256]{3,2,1,0:T(8,128)(2,1)S(1)}, u32[]{:S(2)}, u32[]{:S(2)}) %collective-permute-start) | collective-permute-done | bytes 1048608 | tf_op jit(solution)/shard_map/ppermute | solution.py:309
  25.7 2.0 %add_convert_fusion = bf16[16,2,64,256]{3,2,1,0:T(8,128)(2,1)S(1)} fusion(f32[16,2,64,256]{3,2,1,0:T(8,128)} %get-tuple-element.5, bf16[16,2,64,256]{3,2,1,0:T(8,128)(2,1)S(1)} %collective-permute-done), kind=kLoop, calls=%fused_computation.1 | loop fusion | flops 1572864 | bytes 4194304 | tf_op jit(solution)/shard_map/convert_element_type | solution.py:310
  27.7 23.7 %all_to_all.10 = bf16[16,2,64,256]{3,2,1,0:T(8,128)(2,1)S(1)} all-to-all(bf16[16,2,64,256]{3,2,1,0:T(8,128)(2,1)S(1)} %add_convert_fusion), channel_id=1, replica_groups=mesh['dom'=16,'sub'=8] {'dom'}, dimensions={0} | all-to-all | bytes 2097152 | tf_op jit(solution)/shard_map/all_to_all | solution.py:311
  51.4 0.1 convert_reduce_fusion
  51.6 2.5 %collective-permute-start.3 = (bf16[2,64,256]{2,1,0:T(8,128)(2,1)S(1)}, bf16[2,64,256]{2,1,0:T(8,128)(2,1)S(1)}, u32[]{:S(2)}, u32[]{:S(2)}) collective-permute-start(bf16[2,64,256]{2,1,0:T(8,128)(2,1)S(1)} %convert_element_type.27), channel_id=1, source_target_pairs={{0,6},{1,7},{2,0},{3,1},{4,2},{5,3},{6,4},{7,5},{8,14},{9,15},{10,... | collective-permute-start | bytes 196616 | tf_op jit(solution)/shard_map/ppermute | solution.py:315
  54.1 0.5 collective-permute-start.2
  54.6 0.6 collective-permute-start.1
  55.2 0.2 collective-permute-done.3
  55.4 3.3 %collective-permute-done.2 = bf16[2,64,256]{2,1,0:T(8,128)(2,1)S(1)} collective-permute-done((bf16[2,64,256]{2,1,0:T(8,128)(2,1)S(1)}, bf16[2,64,256]{2,1,0:T(8,128)(2,1)S(1)}, u32[]{:S(2)}, u32[]{:S(2)}) %collective-permute-start.2) | collective-permute-done | bytes 65568 | tf_op jit(solution)/shard_map/ppermute | solution.py:315
  58.8 0.7 collective-permute-done.1
  59.5 0.1 broadcast_in_dim.14
  59.6 16.8 %all_to_all.11.mine_ref = bf16[16,2,64,256]{3,2,1,0:T(8,128)(2,1)S(1)} all-to-all(bf16[16,2,64,256]{3,2,1,0:T(8,128)(2,1)S(1)} %broadcast_in_dim.14), channel_id=1, replica_groups=mesh['dom'=16,'sub'=8] {'dom'}, dimensions={0} | all-to-all | bytes 2097152 | tf_op jit(solution)/shard_map/all_to_all | solution.py:317
  76.4 0.0 copy-start
  76.4 4.8 %collective-permute-start.4 = (bf16[16,2,64,256]{3,2,1,0:T(8,128)(2,1)S(1)}, bf16[16,2,64,256]{3,2,1,0:T(8,128)(2,1)S(1)}, u32[]{:S(2)}, u32[]{:S(2)}) collective-permute-start(bf16[16,2,64,256]{3,2,1,0:T(8,128)(2,1)S(1)} %all_to_all.11.mine_ref), channel_id=1, source_target_pairs={{0,1},{1,0},{2,3},{3,2},{4,5},{5,4},{6,7},{7,6},{8,9},{9,8},{10,11... | collective-permute-start | bytes 3145736 | tf_op jit(solution)/shard_map/ppermute | solution.py:318
  81.2 2.3 %collective-permute-done.4.theirs_ref = bf16[16,2,64,256]{3,2,1,0:T(8,128)(2,1)S(1)} collective-permute-done((bf16[16,2,64,256]{3,2,1,0:T(8,128)(2,1)S(1)}, bf16[16,2,64,256]{3,2,1,0:T(8,128)(2,1)S(1)}, u32[]{:S(2)}, u32[]{:S(2)}) %collective-permute-start.4) | collective-permute-done | bytes 1048608 | tf_op jit(solution)/shard_map/ppermute | solution.py:318
  83.5 0.0 copy-start.1
  83.5 0.0 copy-done
  83.5 1.0 copy-done.1
  84.4 31.9 %gradient.1 = (f32[512,1152]{1,0:T(8,128)}, f32[3,512]{1,0:T(4,128)}) custom-call(f32[3]{0:T(128)} %box_ref.3, bf16[512,1152]{1,0:T(8,128)(2,1)} %charges_ref.3, s32[1,128]{1,0:T(1,128)} %bitcast.3, s32[3,4096]{1,0:T(4,128)} %miller_ref.3, bf16[16,2,64,256]{3,2,1,0:T(8,128)(2,1)} %copy-done, bf16[16,2,64,256]{3,2,1,0:T(8,128)(2,1)} %copy-done.1, ...), custom_call_target="tpu_custom_call" | custom-call | tf_op jit(solution)/shard_map/gradient/pallas_call | solution.py:320
  (2 shorter events, 0.0 us)
Async XLA Ops:
  21.8 3.9 %collective-permute-start = (bf16[16,2,64,256]{3,2,1,0:T(8,128)(2,1)}, bf16[16,2,64,256]{3,2,1,0:T(8,128)(2,1)S(1)}, u32[]{:S(2)}, u32[]{:S(2)}) collective-permute-start(bf16[16,2,64,256]{3,2,1,0:T(8,128)(2,1)} %get-tuple-element.6), channel_id=1, source_target_pairs={{0,1},{1,0},{2,3},{3,2},{4,5},{5,4},{6,7},{7,6},{8,9},{9,8},{10,11... | collective-permute-start | bytes 3145736 | tf_op jit(solution)/shard_map/ppermute | solution.py:309
  51.6 3.9 %collective-permute-start.3 = (bf16[2,64,256]{2,1,0:T(8,128)(2,1)S(1)}, bf16[2,64,256]{2,1,0:T(8,128)(2,1)S(1)}, u32[]{:S(2)}, u32[]{:S(2)}) collective-permute-start(bf16[2,64,256]{2,1,0:T(8,128)(2,1)S(1)} %convert_element_type.27), channel_id=1, source_target_pairs={{0,6},{1,7},{2,0},{3,1},{4,2},{5,3},{6,4},{7,5},{8,14},{9,15},{10,... | collective-permute-start | bytes 196616 | tf_op jit(solution)/shard_map/ppermute | solution.py:315
  54.1 4.7 %collective-permute-start.2 = (bf16[2,64,256]{2,1,0:T(8,128)(2,1)S(1)}, bf16[2,64,256]{2,1,0:T(8,128)(2,1)S(1)}, u32[]{:S(2)}, u32[]{:S(2)}) collective-permute-start(bf16[2,64,256]{2,1,0:T(8,128)(2,1)S(1)} %convert_element_type.27), channel_id=1, source_target_pairs={{0,4},{1,5},{2,6},{3,7},{4,0},{5,1},{6,2},{7,3},{8,12},{9,13},{10,... | collective-permute-start | bytes 196616 | tf_op jit(solution)/shard_map/ppermute | solution.py:315
  54.6 4.8 %collective-permute-start.1 = (bf16[2,64,256]{2,1,0:T(8,128)(2,1)S(1)}, bf16[2,64,256]{2,1,0:T(8,128)(2,1)S(1)}, u32[]{:S(2)}, u32[]{:S(2)}) collective-permute-start(bf16[2,64,256]{2,1,0:T(8,128)(2,1)S(1)} %convert_element_type.27), channel_id=1, source_target_pairs={{0,2},{1,3},{2,4},{3,5},{4,6},{5,7},{6,0},{7,1},{8,10},{9,11},{10,... | collective-permute-start | bytes 196616 | tf_op jit(solution)/shard_map/ppermute | solution.py:315
  76.4 7.1 %copy-start = (bf16[16,2,64,256]{3,2,1,0:T(8,128)(2,1)}, bf16[16,2,64,256]{3,2,1,0:T(8,128)(2,1)S(1)}, u32[]{:S(2)}) copy-start(bf16[16,2,64,256]{3,2,1,0:T(8,128)(2,1)S(1)} %all_to_all.11.mine_ref) | copy-start | bytes 3145732
  76.4 7.1 %collective-permute-start.4 = (bf16[16,2,64,256]{3,2,1,0:T(8,128)(2,1)S(1)}, bf16[16,2,64,256]{3,2,1,0:T(8,128)(2,1)S(1)}, u32[]{:S(2)}, u32[]{:S(2)}) collective-permute-start(bf16[16,2,64,256]{3,2,1,0:T(8,128)(2,1)S(1)} %all_to_all.11.mine_ref), channel_id=1, source_target_pairs={{0,1},{1,0},{2,3},{3,2},{4,5},{5,4},{6,7},{7,6},{8,9},{9,8},{10,11... | collective-permute-start | bytes 3145736 | tf_op jit(solution)/shard_map/ppermute | solution.py:318
  83.5 1.0 copy-start.1

commit v3 on v2

v3 whole, which is shorter than its diff:
```python
import functools
import math

import jax
import jax.numpy as jnp
from jax import lax
from jax.experimental import pallas as pl
from jax.experimental.pallas import tpu as pltpu
from jax.sharding import PartitionSpec as P

TWO_PI = 2.0 * math.pi
ROOT_THREE = math.sqrt(3.0)
MULT = 9
ODD = (1, 2, 3)
VMEM_LIMIT = 24 * 2**20
PHASE_ROWS = 32
TURNED_ROWS = 32
WITH_CHUNKS = 1
LEAD = 0.5
SUM_CHUNKS = 4

SIN_TERMS = (
    4.442883014678955,
    -7.308241367340088,
    3.6062889099121094,
    -0.8457635641098022,
    0.10920575261116028,
)
COS_TERMS = (
    1.4142135381698608,
    -6.978850841522217,
    5.7394609451293945,
    -1.8835630416870117,
    0.31069818139076233,
)


def series(terms, x):
    total = terms[-1]
    for term in terms[-2::-1]:
        total = total * x + term
    return total


def turned(turns):
    rest = turns - jnp.round(turns)
    square = rest * rest
    half_sin = rest * series(SIN_TERMS, square)
    half_cos = series(COS_TERMS, square)
    cosine = 1.0 - half_sin * half_sin
    sine = half_sin * half_cos
    return cosine.astype(jnp.bfloat16), sine.astype(jnp.bfloat16)


def squared_k(numbers, box_ref):
    parts = [TWO_PI * numbers[x] / box_ref[x] for x in range(3)]
    return parts, parts[0] * parts[0] + parts[1] * parts[1] + parts[2] * parts[2]


def harmonic_rows(numbers, box_ref):
    parts, k_square = squared_k(numbers, box_ref)
    inverse = 1.0 / jnp.sqrt(k_square)
    ux, uy, uz = (part * inverse for part in parts)
    rows = {
        0: None,
        1: ux,
        2: uy,
        3: uz,
        4: -ROOT_THREE * ux * uy,
        5: -ROOT_THREE * uy * uz,
        6: -ROOT_THREE * uz * ux,
        7: -0.5 * ROOT_THREE * (ux * ux - uy * uy),
        8: -0.5 * (3.0 * uz * uz - 1.0),
    }
    return rows, k_square


def times(row, x):
    return x if row is None else row * x


def number_rows(miller_ref, start, width):
    return [
        miller_ref[x : x + 1, pl.ds(start, width)].astype(jnp.float32) for x in range(3)
    ]


def run_together(*writers):
    placed = []
    for order, pieces in enumerate(writers):
        whole_cost = sum(cost for cost, _ in pieces)
        done = 0.0
        for cost, piece in pieces:
            placed.append(((done + LEAD * cost) / whole_cost, order, len(placed), piece))
            done += cost
    for entry in sorted(placed, key=lambda entry: entry[:3]):
        entry[3]()


def live_rows(counts, me, shape, dim):
    lane = lax.broadcasted_iota(jnp.int32, counts.shape, 1)
    mine = jnp.sum(jnp.where(lane == me, counts, 0), axis=1, keepdims=True)
    return lax.broadcasted_iota(jnp.int32, shape, dim) < mine


def my_device():
    return lax.axis_index("dom") * lax.axis_size("sub") + lax.axis_index("sub")


def my_core():
    return lax.rem(lax.axis_index("sub"), 2)


def structure_kernel(
    k_block,
    box_ref,
    charges_ref,
    frac_ref,
    counts_ref,
    miller_ref,
    cotangent_ref,
    mine_ref,
    theirs_ref,
    phases_ref,
    charges_t,
    columns,
    gain,
    turns_0,
    turns_1,
    phases_0,
    phases_1,
    sums_0,
    sums_1,
    table_0,
    table_1,
):
    step = pl.program_id(0)
    rows, width = charges_ref.shape
    channels = width // MULT
    half = channels // 2
    k_count = miller_ref.shape[1]
    lanes = k_block // 128
    core = my_core()

    def block_numbers(block):
        start = pl.multiple_of(jnp.clip(block * k_block, 0, k_count - k_block), k_block)
        return number_rows(miller_ref, start, k_block)

    def write_turns(block, turns):
        numbers = block_numbers(block)
        blank = jnp.zeros((10, k_block), jnp.float32)
        both = jnp.concatenate(numbers + numbers + [blank], axis=0).astype(jnp.bfloat16)
        turns[...] = jnp.dot(columns[...], both, preferred_element_type=jnp.float32)

    def write_phases(turns, phases):
        def piece_at(at):
            piece = slice(at, at + PHASE_ROWS)
            cosine, sine = turned(turns[piece, :])
            phases[piece, :k_block] = cosine
            phases[piece, k_block:] = sine

        return [(1, functools.partial(piece_at, at)) for at in range(0, rows, PHASE_ROWS)]

    def write_sums(phases, sums):
        chunk = width // SUM_CHUNKS

        def piece_at(at, kind):
            piece = slice(at, at + chunk)
            sums[kind, piece, :] = jnp.dot(
                charges_t[piece, :],
                phases[:, kind * k_block : (kind + 1) * k_block],
                preferred_element_type=jnp.float32,
            )

        return [
            (1, functools.partial(piece_at, at, kind))
            for at in range(0, width, chunk)
            for kind in range(2)
        ]

    def write_table(block, rows_ref):
        table, k_square = harmonic_rows(block_numbers(block), box_ref)
        rows_ref[0:1, :] = jnp.exp(-0.5 * k_square) / k_square
        for m in range(1, MULT):
            rows_ref[m : m + 1, :] = table[m]

    def write_shares(table, sums):
        def parts_at(at):
            for m in range(MULT):
                with_cos = sums[0, m * channels + at : m * channels + at + 16, :]
                with_sin = sums[1, m * channels + at : m * channels + at + 16, :]
                if m == 0:
                    real, imag = with_cos, with_sin
                    continue
                row = table[m : m + 1, :]
                if m in ODD:
                    real, imag = real - row * with_sin, imag + row * with_cos
                else:
                    real, imag = real + row * with_cos, imag + row * with_sin
            scale = gain[at : at + 16, :] * table[0:1, :]
            return real * scale, imag * scale

        def piece_at(at):
            pairs = zip(parts_at(at), parts_at(half + at))
            for kind, (low, high) in enumerate(pairs):
                mine = jnp.where(core == 0, low, high)
                theirs = jnp.where(core == 0, high, low)
                for lane in range(lanes):
                    first = (kind * lanes + lane) * half + at
                    piece = slice(lane * 128, (lane + 1) * 128)
                    mine_ref[0, first : first + 16, :] = mine[:, piece]
                    theirs_ref[0, first : first + 16, :] = theirs[:, piece].astype(jnp.bfloat16)

        return [(1, functools.partial(piece_at, at)) for at in range(0, half, 16)]

    @pl.when(step == 0)
    def _():
        counts = counts_ref[...]
        total = jnp.sum(counts, axis=1, keepdims=True).astype(jnp.float32)
        live = live_rows(counts, my_device(), (1, rows), 1).astype(jnp.bfloat16)
        charges_t[...] = charges_ref[...].T * live
        coords = frac_ref[...]
        coarse = coords.astype(jnp.bfloat16).astype(jnp.float32)
        fine = (coords - coarse).astype(jnp.bfloat16).astype(jnp.float32)
        padded = jnp.concatenate([coarse, fine, jnp.zeros((10, rows), jnp.float32)], axis=0)
        columns[...] = padded.T.astype(jnp.bfloat16)
        all_numbers = number_rows(miller_ref, 0, k_count)
        _, all_square = squared_k(all_numbers, box_ref)
        all_filter = jnp.exp(-0.5 * all_square) / all_square
        norm = jnp.sqrt(jnp.sum(all_filter * all_filter, axis=1, keepdims=True))
        cotangent = jnp.broadcast_to(cotangent_ref[...], (8, channels)).T[:, 0:1]
        gain[...] = cotangent / (norm * jnp.sqrt(total))
        write_turns(0, turns_0)
        write_turns(1, turns_1)
        run_together(write_phases(turns_0, phases_0))

    turns, phases, sums = (turns_0, turns_1), (phases_0, phases_1), (sums_0, sums_1)
    tables = (table_0, table_1)
    last = pl.num_programs(0) - 1

    for now in range(2):
        other = 1 - now

        @pl.when((step < last) & (lax.rem(step, 2) == now))
        def _(now=now, other=other):
            write_turns(step + 2, turns[now])
            write_table(step, tables[now])
            phases_ref[0] = phases[now][...]
            run_together(
                write_sums(phases[now], sums[now]),
                write_phases(turns[other], phases[other]),
                write_shares(tables[other], sums[other]),
            )

    @pl.when(step == last)
    def _():
        run_together(write_shares(table_1, sums_1))


def gradient_kernel(
    k_block,
    box_ref,
    charges_ref,
    counts_ref,
    miller_ref,
    mine_ref,
    theirs_ref,
    phases_ref,
    before_ref,
    grad_q_ref,
    grad_f_ref,
    turned_by,
    coef_0,
    coef_1,
    with_0,
    with_1,
):
    step = pl.program_id(0)
    last = pl.num_programs(0) - 1
    rows, width = charges_ref.shape
    channels = width // MULT
    half = channels // 2
    k_count = miller_ref.shape[1]
    lanes = k_block // 128
    core = my_core()
    contract = (((1,), (1,)), ((), ()))

    def block_numbers(block):
        start = pl.multiple_of(jnp.clip(block * k_block, 0, k_count - k_block), k_block)
        return number_rows(miller_ref, start, k_block)

    def write_coefs(block, coef):
        table, _ = harmonic_rows(block_numbers(block), box_ref)

        def wide(kind, at):
            low, high = [], []
            for lane in range(lanes):
                first = (kind * lanes + lane) * half + at
                mine = mine_ref[0, first : first + 16, :].astype(jnp.float32)
                theirs = theirs_ref[0, first : first + 16, :].astype(jnp.float32)
                low.append(jnp.where(core == 0, mine, theirs))
                high.append(jnp.where(core == 0, theirs, mine))
            return jnp.concatenate(low, axis=1), jnp.concatenate(high, axis=1)

        def piece_at(at):
            for place, real, imag in zip((at, half + at), wide(0, at), wide(1, at)):
                for m in range(MULT):
                    piece = slice(m * channels + place, m * channels + place + 16)
                    first, second = (imag, -real) if m in ODD else (real, imag)
                    coef[piece, :k_block] = times(table[m], first).astype(jnp.bfloat16)
                    coef[piece, k_block:] = times(table[m], second).astype(jnp.bfloat16)

        return [(1, functools.partial(piece_at, at)) for at in range(0, half, 16)]

    def write_dots(coef, dots):
        part = rows // WITH_CHUNKS

        def with_at(at, kind):
            piece = slice(at, at + part)
            dots[kind, piece, :] = jnp.dot(
                charges_ref[piece, :],
                coef[:, kind * k_block : (kind + 1) * k_block],
                preferred_element_type=jnp.float32,
            )

        def grad_at(at):
            piece = slice(at, min(at + 256, width))
            grad_q_ref[:, piece] += lax.dot_general(
                phases_ref[0], coef[piece, :], contract, preferred_element_type=jnp.float32
            )

        return [
            (5 / WITH_CHUNKS, functools.partial(with_at, at, kind))
            for kind in range(2)
            for at in range(0, rows, part)
        ] + [(2, functools.partial(grad_at, at)) for at in range(0, width, 256)]

    def write_turned(block, dots):
        numbers = block_numbers(block)

        def piece_at(at):
            piece = slice(at, at + TURNED_ROWS)
            cosine = before_ref[0, piece, :k_block].astype(jnp.float32)
            sine = before_ref[0, piece, k_block:].astype(jnp.float32)
            turning = cosine * dots[1, piece, :] - sine * dots[0, piece, :]
            for x in range(3):
                moved = turning * numbers[x]
                folded = moved[:, 0:128]
                for lane in range(1, lanes):
                    folded = folded + moved[:, lane * 128 : (lane + 1) * 128]
                turned_by[x, piece, :] += folded

        return [(1, functools.partial(piece_at, at)) for at in range(0, rows, TURNED_ROWS)]

    coefs, dots = (coef_0, coef_1), (with_0, with_1)

    @pl.when(step == 0)
    def _():
        grad_q_ref[...] = jnp.zeros_like(grad_q_ref)
        turned_by[...] = jnp.zeros_like(turned_by)
        with_1[...] = jnp.zeros_like(with_1)
        run_together(write_coefs(0, coef_0))

    for now in range(2):
        other = 1 - now

        @pl.when((step > 0) & (step < last) & (lax.rem(step, 2) == now))
        def _(now=now, other=other):
            run_together(
                write_dots(coefs[other], dots[other]),
                write_turned(step - 2, dots[now]),
                write_coefs(step, coefs[now]),
            )

    @pl.when(step == last)
    def _():
        run_together(write_turned(step - 2, with_1))
        live = live_rows(counts_ref[...], my_device(), (rows, 1), 0)
        grad_q_ref[...] = jnp.where(live, grad_q_ref[...], 0.0)
        live_lane = live_rows(counts_ref[...], my_device(), (1, rows), 1)
        for x in range(3):
            moved = TWO_PI * jnp.sum(turned_by[x].T, axis=0, keepdims=True)
            grad_f_ref[x : x + 1, :] = jnp.where(live_lane, moved, 0.0)


def whole(shape):
    return pl.BlockSpec(shape, lambda j: (0,) * len(shape))


SMEM = pl.BlockSpec(memory_space=pltpu.SMEM)


def neighbours(doms, subs, moved):
    return [
        (dom * subs + sub, dom * subs + moved(sub)) for dom in range(doms) for sub in range(subs)
    ]


def local(charges, frac_coords, atom_counts, miller, box, cotangent):
    axes = ("dom", "sub")
    doms = lax.axis_size("dom")
    subs = lax.axis_size("sub")
    rows, width = charges.shape
    channels = width // MULT
    half = channels // 2
    k_count = miller.shape[1]
    k_block = k_count // doms
    counts = atom_counts[None, :]
    lines = 2 * half * k_block // 128
    share = (doms, lines, 128)
    share_late = pl.BlockSpec((1, lines, 128), lambda j: (jnp.maximum(j - 1, 0), 0, 0))
    mine, theirs, phases = pl.pallas_call(
        functools.partial(structure_kernel, k_block),
        grid=(doms + 1,),
        in_specs=[
            SMEM,
            whole((rows, width)),
            whole((3, rows)),
            whole((1, doms * subs)),
            whole((3, k_count)),
            whole((1, channels)),
        ],
        out_specs=[
            share_late,
            share_late,
            pl.BlockSpec((1, rows, 2 * k_block), lambda j: (jnp.minimum(j, doms - 1), 0, 0)),
        ],
        out_shape=[
            jax.ShapeDtypeStruct(share, jnp.float32),
            jax.ShapeDtypeStruct(share, jnp.bfloat16),
            jax.ShapeDtypeStruct((doms, rows, 2 * k_block), jnp.bfloat16),
        ],
        scratch_shapes=[
            pltpu.VMEM((width, rows), jnp.bfloat16),
            pltpu.VMEM((rows, 16), jnp.bfloat16),
            pltpu.VMEM((channels, 1), jnp.float32),
            pltpu.VMEM((rows, k_block), jnp.float32),
            pltpu.VMEM((rows, k_block), jnp.float32),
            pltpu.VMEM((rows, 2 * k_block), jnp.bfloat16),
            pltpu.VMEM((rows, 2 * k_block), jnp.bfloat16),
            pltpu.VMEM((2, width, k_block), jnp.float32),
            pltpu.VMEM((2, width, k_block), jnp.float32),
            pltpu.VMEM((16, k_block), jnp.float32),
            pltpu.VMEM((16, k_block), jnp.float32),
        ],
        compiler_params=pltpu.CompilerParams(vmem_limit_bytes=VMEM_LIMIT),
        name="structure",
    )(box, charges, frac_coords, counts, miller, cotangent[None, :])
    other_core = neighbours(doms, subs, lambda sub: sub ^ 1)
    along_x = [
        neighbours(doms, subs, lambda sub, by=by: (sub + by) % subs) for by in range(2, subs, 2)
    ]
    arrived = lax.ppermute(theirs, axes, other_core)
    on_chip = (mine + arrived.astype(jnp.float32)).astype(jnp.bfloat16)
    arrived = lax.all_to_all(on_chip, "dom", 0, 0, tiled=True)
    summed = jnp.sum(arrived.astype(jnp.float32), axis=0)
    sent = summed.astype(jnp.bfloat16)
    for pairs in along_x:
        summed = summed + lax.ppermute(sent, axes, pairs).astype(jnp.float32)
    factor = summed.astype(jnp.bfloat16)
    mine = lax.all_to_all(jnp.broadcast_to(factor[None], share), "dom", 0, 0, tiled=True)
    theirs = lax.ppermute(mine, axes, other_core)
    share_next = pl.BlockSpec((1, lines, 128), lambda j: (jnp.minimum(j, doms - 1), 0, 0))
    grad_q, grad_f = pl.pallas_call(
        functools.partial(gradient_kernel, k_block),
        grid=(doms + 2,),
        in_specs=[
            SMEM,
            whole((rows, width)),
            whole((1, doms * subs)),
            whole((3, k_count)),
            share_next,
            share_next,
            pl.BlockSpec((1, rows, 2 * k_block), lambda j: (jnp.clip(j - 1, 0, doms - 1), 0, 0)),
            pl.BlockSpec((1, rows, 2 * k_block), lambda j: (jnp.clip(j - 2, 0, doms - 1), 0, 0)),
        ],
        out_specs=[whole((rows, width)), whole((3, rows))],
        out_shape=[
            jax.ShapeDtypeStruct((rows, width), jnp.float32),
            jax.ShapeDtypeStruct((3, rows), jnp.float32),
        ],
        scratch_shapes=[
            pltpu.VMEM((3, rows, 128), jnp.float32),
            pltpu.VMEM((width, 2 * k_block), jnp.bfloat16),
            pltpu.VMEM((width, 2 * k_block), jnp.bfloat16),
            pltpu.VMEM((2, rows, k_block), jnp.float32),
            pltpu.VMEM((2, rows, k_block), jnp.float32),
        ],
        compiler_params=pltpu.CompilerParams(vmem_limit_bytes=VMEM_LIMIT),
        name="gradient",
    )(box, charges, counts, miller, mine, theirs, phases, phases)
    return grad_q, grad_f


def solution(mesh):
    in_specs = (P(("dom", "sub"), None), P(None, ("dom", "sub")), P(), P(), P(), P())
    out_specs = (P(("dom", "sub"), None), P(None, ("dom", "sub")))
    return jax.shard_map(local, mesh=mesh, in_specs=in_specs, out_specs=out_specs, check_vma=False)
```

time: 117 us -> 113 us (0.966)
  Pallas kernels: 53.1 us -> 47.8 us
  local copies, waits for them, and re-layouts: 1.07 us -> 4.97 us
  other arithmetic: 2.18 us -> 0.49 us
    pallas_call x2, Pallas kernels: 53.1 us -> 47.8 us  [the longest x1 29.5 us: local(): pl.pallas_call(functools.partial(gradient_kernel, k_block), grid=(doms +...]
    unnamed x4 -> x16, local copies, waits for them, and re-layouts: 0.96 us -> 4.77 us
    convert_element_type x1, other arithmetic: 1.98 us -> 0.3 us  [local(): on_chip = (mine + arrived.astype(jnp.float32)).astype(jnp.bfloat16)]
where the time goes in v3:
time: 113 us
  Pallas kernels  47.8 us (42%)
  blocking collectives  40.5 us (36%)
  starting transfers between devices  9.91 us (9%)
  waiting for transfers between devices  8.77 us (8%)
  local copies, waits for them, and re-layouts  4.97 us (4%)
    pallas_call x1, Pallas kernels, local(): pl.pallas_call(functools.partial(gradient_kernel, k_block), grid=(doms +...  29.5 us
    all_to_all x1, blocking collectives, local(): arrived = lax.all_to_all(on_chip, 'dom', 0, 0, tiled=True)  23.7 us
    pallas_call x1, Pallas kernels, local(): pl.pallas_call(functools.partial(structure_kernel, k_block), grid=(doms +...  18.3 us
    all_to_all x1, blocking collectives, local(): lax.all_to_all(jnp.broadcast_to(factor[None], share), 'dom', 0, 0, tiled=...  16.8 us
    ppermute x1, starting transfers between devices, local(): theirs = lax.ppermute(mine, axes, other_core)  4.78 us
    unnamed x16, local copies, waits for them, and re-layouts  4.77 us
    ppermute x3, waiting for transfers between devices, local(): summed = summed + lax.ppermute(sent, axes, pairs).astype(jnp.float32)  4.19 us
    ppermute x3, starting transfers between devices, local(): summed = summed + lax.ppermute(sent, axes, pairs).astype(jnp.float32)  3.68 us
  transfers between devices with their start and end apart: 5, of which 5 were waited for; matrix products, arithmetic and copies ran while one was open for 0% of the time, Pallas kernels for 0%

profile of v3, /device:TPU:1, one launch (start us, length us, event | category | flops | bytes accessed | tf_op | source)
XLA Modules:
  0.0 113.1 jit_solution(11599675426035083848)
XLA Ops:
  0.6 0.0 copy-start
  0.6 1.3 %copy-done = bf16[512,1152]{1,0:T(8,128)(2,1)S(1)} copy-done((bf16[512,1152]{1,0:T(8,128)(2,1)S(1)}, bf16[512,1152]{1,0:T(8,128)(2,1)}, u32[]{:S(2)}) %copy-start) | copy-done | bytes 1179672
  1.9 0.0 copy-start.1
  1.9 0.8 copy-done.1
  2.7 0.0 copy-start.3
  2.7 0.7 copy-done.3
  3.4 0.0 copy-start.4
  3.4 0.7 copy-done.4
  4.1 0.0 copy-start.5
  4.1 0.7 copy-done.5
  4.8 0.0 copy-start.7
  4.8 0.7 copy-done.7
  5.4 18.3 %structure.1 = (f32[16,256,128]{2,1,0:T(8,128)S(1)}, bf16[16,256,128]{2,1,0:T(8,128)(2,1)S(1)}, bf16[16,512,512]{2,1,0:T(8,128)(2,1)S(1)}) custom-call(f32[3]{0:T(128)S(1)} %copy-done.4, bf16[512,1152]{1,0:T(8,128)(2,1)S(1)} %copy-done, f32[3,512]{1,0:T(4,128)S(1)} %copy-done.3, s32[1,128]{1,0:T(1,128)S(1)} %bitcast.2, s32[3,4096]{1,0:T(4,128)S(1)} %copy-done.1, ...), custom_call_target="tpu_custom_call" | custom-call | tf_op jit(solution)/shard_map/structure/pallas_call | solution.py:412
  23.7 1.5 %collective-permute-start = (bf16[16,256,128]{2,1,0:T(8,128)(2,1)S(1)}, bf16[16,256,128]{2,1,0:T(8,128)(2,1)S(1)}, u32[]{:S(2)}, u32[]{:S(2)}) collective-permute-start(bf16[16,256,128]{2,1,0:T(8,128)(2,1)S(1)} %get-tuple-element.6), channel_id=1, source_target_pairs={{0,1},{1,0},{2,3},{3,2},{4,5},{5,4},{6,7},{7,6},{8,9},{9,8},{10,11... | collective-permute-start | bytes 3145736 | tf_op jit(solution)/shard_map/ppermute | solution.py:453
  25.1 2.3 %collective-permute-done = bf16[16,256,128]{2,1,0:T(8,128)(2,1)S(1)} collective-permute-done((bf16[16,256,128]{2,1,0:T(8,128)(2,1)S(1)}, bf16[16,256,128]{2,1,0:T(8,128)(2,1)S(1)}, u32[]{:S(2)}, u32[]{:S(2)}) %collective-permute-start) | collective-permute-done | bytes 1048608 | tf_op jit(solution)/shard_map/ppermute | solution.py:453
  27.4 0.3 add_convert_fusion
  27.7 23.7 %all_to_all.10 = bf16[16,256,128]{2,1,0:T(8,128)(2,1)S(1)} all-to-all(bf16[16,256,128]{2,1,0:T(8,128)(2,1)S(1)} %add_convert_fusion), channel_id=1, replica_groups=mesh['dom'=16,'sub'=8] {'dom'}, dimensions={0} | all-to-all | bytes 2097152 | tf_op jit(solution)/shard_map/all_to_all | solution.py:455
  51.4 0.1 convert_reduce_fusion
  51.5 0.0 copy-start.2
  51.6 0.0 copy-start.6
  51.6 2.5 %collective-permute-start.3 = (bf16[256,128]{1,0:T(8,128)(2,1)S(1)}, bf16[256,128]{1,0:T(8,128)(2,1)S(1)}, u32[]{:S(2)}, u32[]{:S(2)}) collective-permute-start(bf16[256,128]{1,0:T(8,128)(2,1)S(1)} %convert_element_type.27), channel_id=1, source_target_pairs={{0,6},{1,7},{2,0},{3,1},{4,2},{5,3},{6,4},{7,5},{8,14},{9,15},{10,... | collective-permute-start | bytes 196616 | tf_op jit(solution)/shard_map/ppermute | solution.py:459
  54.1 0.5 collective-permute-start.2
  54.7 0.6 collective-permute-start.1
  55.3 0.2 collective-permute-done.3
  55.5 3.3 %collective-permute-done.2 = bf16[256,128]{1,0:T(8,128)(2,1)S(1)} collective-permute-done((bf16[256,128]{1,0:T(8,128)(2,1)S(1)}, bf16[256,128]{1,0:T(8,128)(2,1)S(1)}, u32[]{:S(2)}, u32[]{:S(2)}) %collective-permute-start.2) | collective-permute-done | bytes 65568 | tf_op jit(solution)/shard_map/ppermute | solution.py:459
  58.8 0.7 collective-permute-done.1
  59.5 0.2 broadcast_in_dim.14
  59.7 16.8 %all_to_all.11.mine_ref = bf16[16,256,128]{2,1,0:T(8,128)(2,1)S(1)} all-to-all(bf16[16,256,128]{2,1,0:T(8,128)(2,1)S(1)} %broadcast_in_dim.14), channel_id=1, replica_groups=mesh['dom'=16,'sub'=8] {'dom'}, dimensions={0} | all-to-all | bytes 2097152 | tf_op jit(solution)/shard_map/all_to_all | solution.py:461
  76.5 4.8 %collective-permute-start.4 = (bf16[16,256,128]{2,1,0:T(8,128)(2,1)S(1)}, bf16[16,256,128]{2,1,0:T(8,128)(2,1)S(1)}, u32[]{:S(2)}, u32[]{:S(2)}) collective-permute-start(bf16[16,256,128]{2,1,0:T(8,128)(2,1)S(1)} %all_to_all.11.mine_ref), channel_id=1, source_target_pairs={{0,1},{1,0},{2,3},{3,2},{4,5},{5,4},{6,7},{7,6},{8,9},{9,8},{10,11... | collective-permute-start | bytes 3145736 | tf_op jit(solution)/shard_map/ppermute | solution.py:462
  81.3 2.3 %collective-permute-done.4.theirs_ref = bf16[16,256,128]{2,1,0:T(8,128)(2,1)S(1)} collective-permute-done((bf16[16,256,128]{2,1,0:T(8,128)(2,1)S(1)}, bf16[16,256,128]{2,1,0:T(8,128)(2,1)S(1)}, u32[]{:S(2)}, u32[]{:S(2)}) %collective-permute-start.4) | collective-permute-done | bytes 1048608 | tf_op jit(solution)/shard_map/ppermute | solution.py:462
  83.6 0.0 copy-done.2
  83.6 0.0 copy-done.6
  83.6 29.5 %gradient.1 = (f32[512,1152]{1,0:T(8,128)}, f32[3,512]{1,0:T(4,128)}) custom-call(f32[3]{0:T(128)S(1)} %copy-done.4, bf16[512,1152]{1,0:T(8,128)(2,1)S(1)} %copy-done, s32[1,128]{1,0:T(1,128)S(1)} %bitcast.3, s32[3,4096]{1,0:T(4,128)S(1)} %copy-done.2, bf16[16,256,128]{2,1,0:T(8,128)(2,1)S(1)} %all_to_all.11.mine_ref, ...), custom_call_target="tpu_custom_call" | custom-call | tf_op jit(solution)/shard_map/gradient/pallas_call | solution.py:464
  (2 shorter events, 0.0 us)
Async XLA Ops:
  0.6 1.3 %copy-start = (bf16[512,1152]{1,0:T(8,128)(2,1)S(1)}, bf16[512,1152]{1,0:T(8,128)(2,1)}, u32[]{:S(2)}) copy-start(bf16[512,1152]{1,0:T(8,128)(2,1)} %charges_ref.3) | copy-start | bytes 3538948
  1.9 0.8 copy-start.1
  2.7 0.7 copy-start.3
  3.4 0.7 copy-start.4
  4.1 0.7 copy-start.5
  4.8 0.7 copy-start.7
  23.7 3.7 %collective-permute-start = (bf16[16,256,128]{2,1,0:T(8,128)(2,1)S(1)}, bf16[16,256,128]{2,1,0:T(8,128)(2,1)S(1)}, u32[]{:S(2)}, u32[]{:S(2)}) collective-permute-start(bf16[16,256,128]{2,1,0:T(8,128)(2,1)S(1)} %get-tuple-element.6), channel_id=1, source_target_pairs={{0,1},{1,0},{2,3},{3,2},{4,5},{5,4},{6,7},{7,6},{8,9},{9,8},{10,11... | collective-permute-start | bytes 3145736 | tf_op jit(solution)/shard_map/ppermute | solution.py:453
  51.5 32.0 %copy-start.2 = (s32[3,4096]{1,0:T(4,128)S(1)}, s32[3,4096]{1,0:T(4,128)}, u32[]{:S(2)}) copy-start(s32[3,4096]{1,0:T(4,128)} %miller_ref.3) | copy-start | bytes 147460
  51.6 32.0 %copy-start.6 = (s32[128]{0:T(128)S(1)}, s32[128]{0:T(128)}, u32[]{:S(2)}) copy-start(s32[128]{0:T(128)} %param.8) | copy-start | bytes 1540
  51.6 3.9 %collective-permute-start.3 = (bf16[256,128]{1,0:T(8,128)(2,1)S(1)}, bf16[256,128]{1,0:T(8,128)(2,1)S(1)}, u32[]{:S(2)}, u32[]{:S(2)}) collective-permute-start(bf16[256,128]{1,0:T(8,128)(2,1)S(1)} %convert_element_type.27), channel_id=1, source_target_pairs={{0,6},{1,7},{2,0},{3,1},{4,2},{5,3},{6,4},{7,5},{8,14},{9,15},{10,... | collective-permute-start | bytes 196616 | tf_op jit(solution)/shard_map/ppermute | solution.py:459
  54.1 4.7 %collective-permute-start.2 = (bf16[256,128]{1,0:T(8,128)(2,1)S(1)}, bf16[256,128]{1,0:T(8,128)(2,1)S(1)}, u32[]{:S(2)}, u32[]{:S(2)}) collective-permute-start(bf16[256,128]{1,0:T(8,128)(2,1)S(1)} %convert_element_type.27), channel_id=1, source_target_pairs={{0,4},{1,5},{2,6},{3,7},{4,0},{5,1},{6,2},{7,3},{8,12},{9,13},{10,... | collective-permute-start | bytes 196616 | tf_op jit(solution)/shard_map/ppermute | solution.py:459
  54.7 4.8 %collective-permute-start.1 = (bf16[256,128]{1,0:T(8,128)(2,1)S(1)}, bf16[256,128]{1,0:T(8,128)(2,1)S(1)}, u32[]{:S(2)}, u32[]{:S(2)}) collective-permute-start(bf16[256,128]{1,0:T(8,128)(2,1)S(1)} %convert_element_type.27), channel_id=1, source_target_pairs={{0,2},{1,3},{2,4},{3,5},{4,6},{5,7},{6,0},{7,1},{8,10},{9,11},{10,... | collective-permute-start | bytes 196616 | tf_op jit(solution)/shard_map/ppermute | solution.py:459
  76.5 7.1 %collective-permute-start.4 = (bf16[16,256,128]{2,1,0:T(8,128)(2,1)S(1)}, bf16[16,256,128]{2,1,0:T(8,128)(2,1)S(1)}, u32[]{:S(2)}, u32[]{:S(2)}) collective-permute-start(bf16[16,256,128]{2,1,0:T(8,128)(2,1)S(1)} %all_to_all.11.mine_ref), channel_id=1, source_target_pairs={{0,1},{1,0},{2,3},{3,2},{4,5},{5,4},{6,7},{7,6},{8,9},{9,8},{10,11... | collective-permute-start | bytes 3145736 | tf_op jit(solution)/shard_map/ppermute | solution.py:462
